TPU v7x, 256 devices: a whole 4x4x8 slice. The times are simulated.
256 devices in a mesh: row: 4 (over x), col: 64 (over y, z, core).
Axes of the slice: x: 4, y: 4, z: 8, core: 2. Of those that a mesh axis runs over, the one named last changes fastest.
Arguments:
- state: float32 [3, 10, 1048576], P(None, None, ('row', 'col')), may hold values from -6 to 6
- depth: float32 [1048576], P(('row', 'col')), may hold values from 1 to 18
- metric: float32 [4, 1048576], P(None, ('row', 'col')), may hold values from -4 to 4, as said below
- partner: int32 [1048576], P(('row', 'col')), may hold values from -63 to 63, as said below
- refine: int32 [1048576], P(('row', 'col')), may hold values from 0 to 1, as said below
- diff_ops: float32 [2, 10, 10], replicated, may hold values from -2 to 2
- lift: float32 [10, 12], replicated, may hold values from -1.75 to 1.75
- prolong: float32 [2, 10, 10], replicated, may hold values from -2 to 2
Outputs:
- refined: float32 [3, 10, 1572864], P(None, None, ('row', 'col'))
Inputs may be any that keep to these rules, and one draw needn't show every extreme that they name: `metric`: (r_x, r_y) and (s_x, s_y) are orthogonal and of equal length, between 1 and 4. Where partner[i] is not 0, j = i + partner[i] is a triangle with partner[j] = -partner[i]; an offset of size 63 occurs in every draw. `refine`: split the curve into sections of 4096 consecutive triangles. The refinements before section k number k * 2048 plus an offset between -1024 and 1024, and both ends of that range occur in every draw; all refinements together number 1048576 / 2.
All inputs are finite; a program needn't handle non-finite values.
Results may differ from a plain program's by a relative error of at most 0.000076.
Values sent between devices are 32-bit elements; how exact they have to be, the bound alone decides.
A program may use at most 64 MiB of HBM per device.

v0:
```python
import jax
import jax.numpy as jnp
from jax import lax
from jax.sharding import PartitionSpec as P

RIM = 64


GRAVITY = 9.81
COURANT = 0.5
HIGH = lax.Precision.HIGHEST


def padded(cells, sides, width):
    for axis, dim in sides:
        count = lax.axis_size(axis)
        ends = count - 1
        head = lax.slice_in_dim(cells, 0, width, axis=dim)
        tail = lax.slice_in_dim(cells, cells.shape[dim] - width, cells.shape[dim], axis=dim)
        cells = jnp.concatenate(
            [
                lax.ppermute(tail, axis, [(i, (i + 1) % count) for i in range(ends)]),
                cells,
                lax.ppermute(head, axis, [((i + 1) % count, i) for i in range(ends)]),
            ],
            axis=dim,
        )
    return cells


def entering(value, axis, join, neutral):
    count, mine = (lax.axis_size(axis), lax.axis_index(axis))
    pieces = lax.all_gather(value, axis)
    total = jnp.full_like(value, 0) + jnp.asarray(neutral, value.dtype)

    def hop(position, total):
        longer = join(total, pieces[position])
        return jnp.where(position < mine, longer, total)

    return lax.fori_loop(0, count - 1, hop, total)


def shifted(block, axis, distance):
    devices = range(lax.axis_size(axis))
    route = [(i - distance, i) for i in devices if i - distance in devices]
    return lax.ppermute(block, axis, route)


def apply_ops(matrix, field):
    return jnp.einsum("ab,fbx->fax", matrix, field, precision=HIGH)


def face_rows(field):
    return jnp.concatenate(
        [
            field[:, 0:4],
            field[:, 3:4],
            field[:, 6:7],
            field[:, 8:10],
            field[:, 9:10],
            field[:, 7:8],
            field[:, 4:5],
            field[:, 0:1],
        ],
        axis=1,
    )


def normal_flux(values, speed_sq, normal_x, normal_y):
    return jnp.stack(
        [
            values[1] * normal_x + values[2] * normal_y,
            speed_sq * values[0] * normal_x,
            speed_sq * values[0] * normal_y,
        ]
    )


def face_vectors(metric):
    grad_rx, grad_ry, grad_sx, grad_sy = (metric[0], metric[1], metric[2], metric[3])
    return ((-grad_sx, -grad_sy), (grad_rx + grad_sx, grad_ry + grad_sy), (-grad_rx, -grad_ry))


def wave_rate(depth, metric):
    lengths = [jnp.sqrt(vx * vx + vy * vy) for vx, vy in face_vectors(metric)]
    return jnp.sqrt(GRAVITY * depth) * jnp.maximum(jnp.maximum(lengths[0], lengths[1]), lengths[2])


def tendency(state, depth, metric, outer, outer_depth, walls, diff_ops, lift):
    speed_sq = GRAVITY * depth
    grad_rx, grad_ry, grad_sx, grad_sy = (metric[0], metric[1], metric[2], metric[3])
    moved = jnp.stack([state[1], state[2], state[0]])
    along_r = apply_ops(diff_ops[0], moved)
    along_s = apply_ops(diff_ops[1], moved)
    vol_eta = -(
        grad_rx * along_r[0] + grad_sx * along_s[0] + grad_ry * along_r[1] + grad_sy * along_s[1]
    )
    vol_mx = -speed_sq * (grad_rx * along_r[2] + grad_sx * along_s[2])
    vol_my = -speed_sq * (grad_ry * along_r[2] + grad_sy * along_s[2])
    inner = face_rows(state)
    jumps = []
    for edge_num, (vec_x, vec_y) in enumerate(face_vectors(metric)):
        length = jnp.sqrt(vec_x * vec_x + vec_y * vec_y)
        normal_x = vec_x / length
        normal_y = vec_y / length
        inside = inner[:, 4 * edge_num : 4 * edge_num + 4, :]
        normal_m = inside[1] * normal_x + inside[2] * normal_y
        ghost = jnp.stack(
            [
                inside[0],
                inside[1] - 2.0 * normal_m * normal_x,
                inside[2] - 2.0 * normal_m * normal_y,
            ]
        )
        closed = walls[edge_num]
        outside = jnp.where(closed, ghost, outer[edge_num])
        outside_sq = jnp.where(closed, speed_sq, GRAVITY * outer_depth[edge_num])
        flux_in = normal_flux(inside, speed_sq, normal_x, normal_y)
        flux_out = normal_flux(outside, outside_sq, normal_x, normal_y)
        wave_top = jnp.sqrt(jnp.maximum(speed_sq, outside_sq))
        common = 0.5 * (flux_in + flux_out) - 0.5 * wave_top * (outside - inside)
        jumps.append(length * (flux_in - common))
    surface = apply_ops(lift, jnp.concatenate(jumps, axis=1))
    return jnp.stack([vol_eta, vol_mx, vol_my]) + surface


def add_ints(earlier, later):
    return earlier + later


def window_rows(data, start):
    return lax.dynamic_slice_in_dim(data, start, 128, data.ndim - 1)


def shards(state, depth, metric, partner, refine, diff_ops, lift, prolong):
    cells = state.shape[2]
    nblocks = cells // 128
    reach = 128 + 2 * RIM
    devices = lax.axis_size(("row", "col"))
    place = lax.axis_index(("row", "col"))
    first_cell = place * cells
    index = first_cell + jnp.arange(cells, dtype=jnp.int32)
    top = lax.pmax(jnp.max(wave_rate(depth, metric)), ("row", "col"))
    step = COURANT / top
    walls = (index == 0, index == devices * cells - 1, partner == 0)
    pair_local = jnp.arange(128, dtype=jnp.int32)[None, :] + partner.reshape(nblocks, 128) + RIM

    def neighbours(payload):
        return padded(payload, ((("row", "col"), 1),), RIM)

    def rhs(current):
        own_traces = face_rows(current)
        flat = jnp.concatenate([own_traces.reshape(36, cells), depth[None, :]], axis=0)
        wide = neighbours(flat)
        traces = wide[:36].reshape(3, 12, cells + 2 * RIM)
        depth_wide = wide[36]
        from_prev = traces[:, 7:3:-1, RIM - 1 : RIM - 1 + cells]
        from_next = traces[:, 3::-1, RIM + 1 : RIM + 1 + cells]
        depth_prev = depth_wide[RIM - 1 : RIM - 1 + cells]
        depth_next = depth_wide[RIM + 1 : RIM + 1 + cells]
        pair_src = jnp.concatenate(
            [traces[:, 11:7:-1, :].reshape(12, cells + 2 * RIM), depth_wide[None, :]], axis=0
        )
        main_part = pair_src[:, :cells].reshape(13, nblocks, 128)
        rest = pair_src[:, 128:]
        rest = jnp.concatenate([rest, jnp.zeros((13, 128 - 2 * RIM), jnp.float32)], axis=1)
        tail_part = rest.reshape(13, nblocks, 128)
        windows = jnp.concatenate([main_part, tail_part], axis=2)
        pair_table = (
            pair_local[:, :, None] == lax.broadcasted_iota(jnp.int32, (nblocks, 128, reach), 2)
        ).astype(jnp.float32)
        picked = jnp.einsum("rbw,bjw->rbj", windows, pair_table, precision=HIGH).reshape(13, cells)
        from_pair = picked[:12].reshape(3, 4, cells)
        depth_pair = picked[12]
        return tendency(
            current,
            depth,
            metric,
            (from_prev, from_next, from_pair),
            (depth_prev, depth_next, depth_pair),
            walls,
            diff_ops,
            lift,
        )

    first = state + step * rhs(state)
    second = 0.5 * state + 0.5 * (first + step * rhs(first))
    counts = 1 + refine
    blocks = counts.reshape(-1, 128).astype(jnp.float32)
    row_ids = lax.broadcasted_iota(jnp.int32, (128, 128), 0)
    col_ids = lax.broadcasted_iota(jnp.int32, (128, 128), 1)
    upper = (row_ids <= col_ids).astype(jnp.float32)
    within = jnp.dot(blocks, upper, precision=HIGH, preferred_element_type=jnp.float32)
    block_sums = within[:, -1]
    before = jnp.cumsum(block_sums) - block_sums
    ends = (within + before[:, None]).reshape(-1).astype(jnp.int32)
    starts = ends - counts
    extra = jnp.sum(refine)
    earlier = entering(extra, ("row", "col"), add_ints, jnp.int32(0))
    margin = cells // 2
    share = 3 * cells // 2
    span = share + 2 * margin
    slot_blocks = (span + 127) // 128
    offset = earlier - place * (cells // 2) + margin
    bases = jnp.arange(slot_blocks, dtype=jnp.int32) * 128 - offset
    first_parent = jnp.searchsorted(ends, bases, side="right", method="compare_all")
    win_start = jnp.clip(first_parent, 0, cells - 128)
    child_one = jnp.where(refine == 1, apply_ops(prolong[0], second), second).reshape(30, cells)
    child_two = apply_ops(prolong[1], second).reshape(30, cells)
    data = jnp.concatenate([child_one, child_two], axis=0)
    lanes = jnp.arange(128, dtype=jnp.int32)
    iota_pick = lax.broadcasted_iota(jnp.int32, (128, 128), 1)

    def place_block(inputs):
        base, begin = inputs
        data_win = window_rows(data, begin)
        ends_win = window_rows(ends, begin)
        starts_win = window_rows(starts, begin)
        slots = base + lanes
        local = jnp.sum((ends_win[None, :] <= slots[:, None]).astype(jnp.int32), axis=1)
        local = jnp.minimum(local, 127)
        hit = local[:, None] == iota_pick
        which = slots[:, None] - starts_win[None, :]
        pick_one = (hit & (which == 0)).astype(jnp.float32)
        pick_two = (hit & (which == 1)).astype(jnp.float32)
        return jnp.einsum("ri,pi->rp", data_win[:30], pick_one, precision=HIGH) + jnp.einsum(
            "ri,pi->rp", data_win[30:], pick_two, precision=HIGH
        )

    placed = lax.map(place_block, (bases, win_start))
    canvas = jnp.transpose(placed, (1, 0, 2)).reshape(3, 10, slot_blocks * 128)
    flat_slots = (bases[:, None] + lanes[None, :]).reshape(-1)
    valid = (flat_slots >= 0) & (flat_slots < ends[-1])
    canvas = jnp.where(valid, canvas, 0.0)
    from_after = shifted(canvas[:, :, :margin], ("row", "col"), -1)
    from_before = shifted(canvas[:, :, margin + share :], ("row", "col"), 1)
    middle = canvas[:, :, margin : margin + share]
    middle = middle.at[:, :, share - margin :].add(from_after)
    middle = middle.at[:, :, :margin].add(from_before)
    return middle


def solution(mesh):
    return jax.shard_map(
        shards,
        mesh=mesh,
        in_specs=(
            P(None, None, ("row", "col")),
            P(("row", "col")),
            P(None, ("row", "col")),
            P(("row", "col")),
            P(("row", "col")),
            P(),
            P(),
            P(),
        ),
        out_specs=P(None, None, ("row", "col")),
        check_vma=False,
    )
```

profile of v0, /device:TPU:2, one launch (start us, length us, event | category | flops | bytes accessed | tf_op | source)
XLA Modules:
  0.0 1153.6 jit_solution(16237860170042735533)
XLA Ops:
  3.3 1.9 collective-permute-start
  5.3 9.6 collective-permute-start.1
  23.8 1.8 convolution_bitcast_fusion.7
  27.3 2.1 add_subtract_fusion
  30.1 72.4 %all-reduce = s32[256]{0:T(256)S(1)} all-reduce(s32[256]{0:T(256)S(1)} %dynamic-update-slice.6), channel_id=1, replica_groups=mesh['row'=4,'col'=64] {'row','col'}, use_global_device_ids=true, to_apply=%add | all-reduce | flops 256 | bytes 2048
  102.5 327.6 %while.26 = (s32[]{:T(128)}, s32[]{:T(128)}, s32[]{:T(128)}, s32[256]{0:T(256)S(1)}, s32[]{:T(128)}) while((s32[]{:T(128)}, s32[]{:T(128)}, s32[]{:T(128)}, s32[256]{0:T(256)S(1)}, s32[]{:T(128)}) %tuple.151), condition=%wide.region_2.3_spmd, body=%wide.region_1.0_spmd.sunk | while | flops 5 | bytes 107 | solution.py:40
  434.4 2.2 concatenate.71
  437.6 2.0 reshape.981
  440.6 2.3 fusion.154
  444.8 2.5 fusion.36
  448.1 9.8 rev.18
  462.6 2.2 sqrt_multiply_fusion.5
  464.9 74.5 %pmax.7 = f32[]{:T(128)} all-reduce(f32[]{:T(128)} %get-tuple-element.322), channel_id=1, replica_groups=mesh['row'=4,'col'=64] {'row','col'}, use_global_device_ids=true, to_apply=%region_6.7 | all-reduce | flops 1 | bytes 8 | tf_op jit(solution)/shard_map/pmax | solution.py:143
  560.3 4.1 concatenate.79
  565.8 2.0 collective-permute-start.2
  567.8 8.1 collective-permute-start.3
  584.7 2.2 fusion.153
  590.9 2.5 fusion.37
  603.6 529.8 %while.27 = (s32[]{:T(128)}, f32[80,30,128]{2,1,0:T(8,128)}, s32[80]{0:T(128)S(1)}, f32[60,4096]{1,0:T(8,128)S(1)}, s32[4096]{0:T(1024)}, /*index=5*/s32[80]{0:T...) while((s32[]{:T(128)}, f32[80,30,128]{2,1,0:T(8,128)}, ...), condition=%wide.region_9.10_spmd.clone, body=%wide.region_7.9_spmd.clone.sunk | while | flops 11980678 | bytes 89803 | solution.py:230
  1133.3 2.0 copy.82
  1136.3 2.4 collective-permute-start.4
  1138.8 2.0 collective-permute-start.5
  1140.7 3.2 collective-permute-done.4
  1144.0 8.1 collective-permute-done.5
  (1473 shorter events, 608.5 us)
Async XLA Ops:
  0.0 553.3 %copy-start = (f32[10,12]{1,0:T(8,128)S(1)}, f32[10,12]{1,0:T(8,128)}, u32[]{:S(2)}) copy-start(f32[10,12]{1,0:T(8,128)} %param.22) | copy-start | bytes 1444
  3.3 431.1 %collective-permute-start = (f32[37,64]{1,0:T(8,128)}, f32[37,64]{1,0:T(8,128)}, u32[]{:S(2)}, u32[]{:S(2)}) collective-permute-start(f32[37,64]{1,0:T(8,128)} %get-tuple-element.265), channel_id=1, source_target_pairs={{0,1},{1,2},{2,3},{3,4},{4,5},{5,6},{6,7},{7,8},{8,9},{9,10},{10,1... | collective-permute-start | bytes 28424 | tf_op jit(solution)/shard_map/ppermute | solution.py:22
  5.3 429.2 %collective-permute-start.1 = (f32[37,64]{1,0:T(8,128)}, f32[37,64]{1,0:T(8,128)}, u32[]{:S(2)}, u32[]{:S(2)}) collective-permute-start(f32[37,64]{1,0:T(8,128)} %get-tuple-element.264), channel_id=1, source_target_pairs={{1,0},{2,1},{3,2},{4,3},{5,4},{6,5},{7,6},{8,7},{9,8},{10,9},{11,1... | collective-permute-start | bytes 28424 | tf_op jit(solution)/shard_map/ppermute | solution.py:24
  29.3 408.2 %copy-start.170 = (s32[4096]{0:T(1024)}, s32[4096]{0:T(1024)S(1)}, u32[]{:S(2)}) copy-start(s32[4096]{0:T(1024)S(1)} %get-tuple-element.425) | copy-start | bytes 49156
  433.5 117.4 %copy-start.154 = (pred[4096]{0:T(1024)(128)(4,1)}, pred[4096]{0:T(1024)(128)(4,1)S(1)}, u32[]{:S(2)}) copy-start(pred[4096]{0:T(1024)(128)(4,1)S(1)} %get-tuple-element.335) | copy-start | bytes 12292
  434.4 114.0 %copy-start.109 = (f32[1,4096]{1,0:T(1,128)}, f32[1,4096]{1,0:T(1,128)S(1)}, u32[]{:S(2)}) copy-start(f32[1,4096]{1,0:T(1,128)S(1)} %slice.498) | copy-start | bytes 49156
  447.4 15.2 %copy-start.41 = (f32[1,4096]{1,0:T(1,128)S(1)}, f32[1,4096]{1,0:T(1,128)}, u32[]{:S(2)}) copy-start(f32[1,4096]{1,0:T(1,128)} %get-tuple-element.307) | copy-start | bytes 49156
  447.4 15.2 %copy-start.111 = (f32[1,4096]{1,0:T(1,128)S(1)}, f32[1,4096]{1,0:T(1,128)}, u32[]{:S(2)}) copy-start(f32[1,4096]{1,0:T(1,128)} %get-tuple-element.310) | copy-start | bytes 49156
  447.4 15.2 %copy-start.114 = (f32[1,4096]{1,0:T(1,128)S(1)}, f32[1,4096]{1,0:T(1,128)}, u32[]{:S(2)}) copy-start(f32[1,4096]{1,0:T(1,128)} %get-tuple-element.311) | copy-start | bytes 49156
  448.1 91.2 %copy-start.57 = (f32[1,4096]{1,0:T(1,128)S(1)}, f32[1,4096]{1,0:T(1,128)}, u32[]{:S(2)}) copy-start(f32[1,4096]{1,0:T(1,128)} %copy-done.56) | copy-start | bytes 49156
  448.1 91.2 %copy-start.61 = (f32[1,4096]{1,0:T(1,128)S(1)}, f32[1,4096]{1,0:T(1,128)}, u32[]{:S(2)}) copy-start(f32[1,4096]{1,0:T(1,128)} %copy-done.60) | copy-start | bytes 49156
  462.5 79.1 %copy-start.4 = (f32[3,4,4096]{2,1,0:T(4,128)S(1)}, f32[3,4,4096]{2,1,0:T(4,128)}, u32[]{:S(2)}) copy-start(f32[3,4,4096]{2,1,0:T(4,128)} %rev.18) | copy-start | bytes 589828
  462.5 80.6 %copy-start.8 = (f32[3,4,4096]{2,1,0:T(4,128)S(1)}, f32[3,4,4096]{2,1,0:T(4,128)}, u32[]{:S(2)}) copy-start(f32[3,4,4096]{2,1,0:T(4,128)} %get-tuple-element.333) | copy-start | bytes 589828
  462.5 80.6 %copy-start.49 = (f32[1,4096]{1,0:T(1,128)S(1)}, f32[1,4096]{1,0:T(1,128)}, u32[]{:S(2)}) copy-start(f32[1,4096]{1,0:T(1,128)} %copy-done.48) | copy-start | bytes 49156
  462.6 80.6 %copy-start.53 = (f32[1,4096]{1,0:T(1,128)S(1)}, f32[1,4096]{1,0:T(1,128)}, u32[]{:S(2)}) copy-start(f32[1,4096]{1,0:T(1,128)} %copy-done.52) | copy-start | bytes 49156
  462.6 80.6 %copy-start.148 = (f32[4096]{0:T(1024)S(1)}, f32[4096]{0:T(1024)}, u32[]{:S(2)}) copy-start(f32[4096]{0:T(1024)} %broadcast_multiply_fusion.3) | copy-start | bytes 49156
  464.8 77.5 %copy-start.168 = (f32[4096]{0:T(1024)S(1)}, f32[4096]{0:T(1024)}, u32[]{:S(2)}) copy-start(f32[4096]{0:T(1024)} %get-tuple-element.215) | copy-start | bytes 49156
  565.6 15.2 %copy-start.2 = (f32[3,10,4096]{2,1,0:T(8,128)S(1)}, f32[3,10,4096]{2,1,0:T(8,128)}, u32[]{:S(2)}) copy-start(f32[3,10,4096]{2,1,0:T(8,128)} %convolution_bitcast_fusion.3) | copy-start | bytes 1474564
  565.7 15.2 %copy-start.110 = (f32[1,4096]{1,0:T(1,128)S(1)}, f32[1,4096]{1,0:T(1,128)}, u32[]{:S(2)}) copy-start(f32[1,4096]{1,0:T(1,128)} %copy-done.109) | copy-start | bytes 49156
  565.7 15.2 %copy-start.113 = (f32[1,4096]{1,0:T(1,128)S(1)}, f32[1,4096]{1,0:T(1,128)}, u32[]{:S(2)}) copy-start(f32[1,4096]{1,0:T(1,128)} %get-tuple-element.310) | copy-start | bytes 49156
  565.8 16.1 %collective-permute-start.2 = (f32[37,64]{1,0:T(8,128)S(1)}, f32[37,64]{1,0:T(8,128)S(1)}, u32[]{:S(2)}, u32[]{:S(2)}) collective-permute-start(f32[37,64]{1,0:T(8,128)S(1)} %get-tuple-element.261), channel_id=1, source_target_pairs={{0,1},{1,2},{2,3},{3,4},{4,5},{5,6},{6,7},{7,8},{8,9},{9,10},{10,1... | collective-permute-start | bytes 28424 | tf_op jit(solution)/shard_map/ppermute | solution.py:22
  567.8 14.7 %collective-permute-start.3 = (f32[37,64]{1,0:T(8,128)S(1)}, f32[37,64]{1,0:T(8,128)}, u32[]{:S(2)}, u32[]{:S(2)}) collective-permute-start(f32[37,64]{1,0:T(8,128)S(1)} %get-tuple-element.260), channel_id=1, source_target_pairs={{1,0},{2,1},{3,2},{4,3},{5,4},{6,5},{7,6},{8,7},{9,8},{10,9},{11,1... | collective-permute-start | bytes 28424 | tf_op jit(solution)/shard_map/ppermute | solution.py:24
  1136.3 7.7 collective-permute-start.4
  1138.8 13.3 %collective-permute-start.5 = (f32[3,10,2048]{2,1,0:T(8,128)S(1)}, f32[3,10,2048]{2,1,0:T(8,128)S(1)}, u32[]{:S(2)}, u32[]{:S(2)}) collective-permute-start(f32[3,10,2048]{2,1,0:T(8,128)S(1)} %get-tuple-element.227), channel_id=1, source_target_pairs={{0,1},{1,2},{2,3},{3,4},{4,5},{5,6},{6,7},{7,8},{8,9},{9,10},{10,1... | collective-permute-start | bytes 737288 | tf_op jit(solution)/shard_map/ppermute | solution.py:46
  (164 other events, 563.2 us)
where the time goes:
time: 1170 us; the launch traced here: 1150 us
  local copies, waits for them, and re-layouts  435 us (37%)
  loops' own time  322 us (28%)
  blocking collectives  147 us (13%)
  matrix products  105 us (9%)
  other arithmetic  104 us (9%)
  starting transfers between devices  26 us (2%)
    another operation x1, loops' own time, entering(): return lax.fori_loop(0, count - 1, hop, total)  164 us
    dynamic_slice x255, local copies, waits for them, and re-layouts, hop(): longer = join(total, pieces[position])  163 us
    another operation x1, loops' own time, shards(): placed = lax.map(place_block, (bases, win_start))  157 us
    dynamic_slice x160, local copies, waits for them, and re-layouts, window_rows(): return lax.dynamic_slice_in_dim(data, start, 128, data.ndim - 1)  124 us
    dynamic_slice x160, local copies, waits for them, and re-layouts, shards(): placed = lax.map(place_block, (bases, win_start))  93.1 us
    pmax x1, blocking collectives, shards(): top = lax.pmax(jnp.max(wave_rate(depth, metric)), ('row', 'col'))  74.5 us
    dot_general x80, matrix products, place_block(): jnp.einsum('ri,pi->rp', data_win[30:], pick_two, precision=HIGH)  74 us
    unnamed x1, blocking collectives  72.4 us
  transfers between devices with their start and end apart: 6, of which 2 were waited for; matrix products, arithmetic and copies ran while one was open for 16% of the time, Pallas kernels for 0%

commit v1 on v0

v1 whole, which is shorter than its diff:
```python
import functools

import jax
import jax.numpy as jnp
from jax import lax
from jax.experimental import pallas as pl
from jax.experimental.pallas import tpu as pltpu
from jax.sharding import PartitionSpec as P

GRAVITY = 9.81
COURANT = 0.5
MESH = pl.DeviceIdType.MESH

OWN = 32
HALO = 9
WIDE = HALO * 128
BASE = 24
MEM = 72
QP = 40
RP = 32
XP = 96

FACES = ((0, 1, 2, 3), (3, 6, 8, 9), (9, 7, 4, 0))
MEET = ((9, 8, 6, 3), (3, 2, 1, 0), (0, 4, 7, 9))

f32 = jnp.float32
bf16 = jnp.bfloat16
i32 = jnp.int32


def lanes_of(shape):
    return lax.broadcasted_iota(i32, shape, len(shape) - 1)


def state_row(f, n):
    return 4 * n + f


def result_row(f, n):
    return 10 * f + n


def spread(ref, v, tile, pitch):
    return ref[pl.ds(tile * pitch + v, 8, stride=pitch), :]


def put(ref, v, tile, pitch, value):
    ref[pl.ds(tile * pitch + v, 8, stride=pitch), :] = value


def pick(x, idx):
    return jnp.take_along_axis(x, idx, axis=1, mode="promise_in_bounds")


def split(x):
    hi = x.astype(bf16)
    return hi, (x - hi.astype(f32)).astype(bf16)


def exchange(
    rows, cols, low,
    state, metric, depth, partner, refine,
    ls, lm, ld, lp, lr, rs, rm, rd, rp, rr, stat,
    mt, mine, box1, pair2, box2, send, recv, send1, recv1, send2, recv2,
):
    total = rows * cols
    high = total // low
    me = lax.axis_index("row") * cols + lax.axis_index("col")
    lo, hi = lax.rem(me, low), me // low

    def at(flat):
        return (flat // cols, lax.rem(flat, cols))

    right = at(lax.rem(me + 1, total))
    left = at(lax.rem(me + total - 1, total))
    peers1 = [at(hi * low + lax.rem(lo + d, low)) for d in range(1, low)]
    peers2 = [at(lax.rem(hi + d, high) * low + lo) for d in range(1, high)]

    barrier = pltpu.get_barrier_semaphore()
    everyone = [left, right] + peers1 + peers2
    for peer in everyone:
        pl.semaphore_signal(barrier, inc=1, device_id=peer, device_id_type=MESH)

    for t in range(OWN):
        mt[t * 8 : t * 8 + 4, :] = metric[:, t * 128 : (t + 1) * 128]
    grads = [mt[pl.ds(k, OWN, stride=8), :] for k in range(4)]
    rate = wave_rate(depth[...], grads)
    top = jnp.max(jnp.max(rate, axis=1, keepdims=True), axis=0, keepdims=True)
    count = refine[...].astype(f32)
    count = jnp.sum(jnp.sum(count, axis=1, keepdims=True), axis=0, keepdims=True)
    first_row = lax.broadcasted_iota(i32, (8, 128), 0) == 0
    mine[...] = jnp.where(first_row, top, count)

    pl.semaphore_wait(barrier, len(everyone))

    copies = []
    sides = (
        (right, (state.at[:, :, pl.ds((OWN - HALO) * 128, WIDE)], metric.at[:, pl.ds((OWN - HALO) * 128, WIDE)],
                 depth.at[pl.ds(16, 16)], partner.at[pl.ds(16, 16)], refine.at[pl.ds(16, 16)]), (ls, lm, ld, lp, lr)),
        (left, (state.at[:, :, pl.ds(0, WIDE)], metric.at[:, pl.ds(0, WIDE)],
                depth.at[pl.ds(0, 16)], partner.at[pl.ds(0, 16)], refine.at[pl.ds(0, 16)]), (rs, rm, rd, rp, rr)),
    )
    for peer, sources, targets in sides:
        for source, target in zip(sources, targets):
            k = len(copies)
            copies.append(pltpu.make_async_remote_copy(
                src_ref=source, dst_ref=target, send_sem=send.at[k], recv_sem=recv.at[k],
                device_id=peer, device_id_type=MESH))
    for copy in copies:
        copy.start()

    def round_of(source, box, peers, sems, rems):
        batch = [
            pltpu.make_async_remote_copy(
                src_ref=source, dst_ref=box.at[d], send_sem=sems.at[d], recv_sem=rems.at[d],
                device_id=peer, device_id_type=MESH)
            for d, peer in enumerate(peers)
        ]
        for copy in batch:
            copy.start()
        for copy in batch:
            copy.wait()

    def joined(own, box, size, position):
        best, both, before = own, own, jnp.zeros_like(own)
        for d in range(size - 1):
            part = box[d]
            best = jnp.maximum(best, part)
            both = both + part
            before = before + jnp.where(d + 1 <= position, part, 0.0)
        return best, both, before

    round_of(mine, box1, peers1, send1, recv1)
    best, both, before1 = joined(mine[...], box1, low, lo)
    pair2[...] = jnp.where(first_row, best, both)
    round_of(pair2, box2, peers2, send2, recv2)
    best, _, before2 = joined(pair2[...], box2, high, hi)
    offset = before1 + before2 - (me * (OWN * 64)).astype(f32)
    stat[...] = jnp.where(first_row, best, offset)
    for copy in copies:
        copy.wait()


def wave_rate(depth, grads):
    gx, gy, hx, hy = grads
    lengths = [jnp.sqrt(vx * vx + vy * vy) for vx, vy in ((hx, hy), (gx + hx, gy + hy), (gx, gy))]
    return jnp.sqrt(GRAVITY * depth) * jnp.maximum(jnp.maximum(lengths[0], lengths[1]), lengths[2])


def load_tiles(own, left, right, qt, mt, cv, pv, ends):
    state, metric, depth, partner = own
    ls, lm, ld, lp = left
    rs, rm, rd, rp = right

    def lay(m, s, g, t):
        here = slice(t * 128, (t + 1) * 128)
        for n in range(10):
            qt[m * QP + 4 * n : m * QP + 4 * n + 3, :] = s[n, :, here]
        mt[m * 8 : m * 8 + 4, :] = g[:, here]

    for t in range(OWN):
        lay(BASE + t, state, metric, t)
    for t in range(HALO):
        lay(BASE - HALO + t, ls, lm, t)
        if t < HALO - 1:
            lay(BASE + OWN + t, rs, rm, t)
    lay(8, rs, rm, HALO - 1)
    lay(64, rs, rm, HALO - 1)
    lay(7, rs, rm, HALO - 2)
    for into, mid, before, after in ((cv, depth, ld, rd), (pv, partner, lp, rp)):
        into[BASE : BASE + OWN, :] = mid[...]
        into[BASE - HALO : BASE, :] = before[16 - HALO : 16, :]
        into[BASE + OWN : BASE + OWN + 8, :] = after[0:8, :]
        into[7:8, :] = after[7:8, :]
        into[8:9, :] = after[8:9, :]
        into[64:65, :] = after[8:9, :]
    first, last = ends

    @pl.when(first)
    def _():
        cv[BASE - 1 : BASE, :] = pltpu.roll(cv[BASE : BASE + 1, :], 127, 1)

    @pl.when(last)
    def _():
        cv[BASE + OWN : BASE + OWN + 1, :] = pltpu.roll(cv[BASE + OWN - 1 : BASE + OWN, :], 1, 1)

    cv[...] = GRAVITY * cv[...]


def mirror(src, pitch, at, mt, ends):
    lane = lanes_of((1, 128))

    def row(tile, v):
        return src[tile * pitch + v : tile * pitch + v + 1, :]

    def grads(tile):
        return [mt[tile * 8 + k : tile * 8 + k + 1, :] for k in range(4)]

    def write(tile, rim, nodes, meet, gx, gy, shift, target):
        length = jnp.sqrt(gx * gx + gy * gy)
        nx, ny = gx / length, gy / length
        for j in range(4):
            eta, mx, my = (row(tile, at(f, nodes[j])) for f in range(3))
            normal = mx * nx + my * ny
            for f, value in enumerate((eta, mx - 2.0 * normal * nx, my - 2.0 * normal * ny)):
                v = at(f, meet[j])
                old = row(rim, v)
                src[rim * pitch + v : rim * pitch + v + 1, :] = jnp.where(
                    lane == target, pltpu.roll(value, shift, 1), old)

    first, last = ends

    @pl.when(first)
    def _():
        _, _, sx, sy = grads(BASE)
        write(BASE, BASE - 1, FACES[0], MEET[0], -sx, -sy, 127, 127)

    @pl.when(last)
    def _():
        rx, ry, sx, sy = grads(BASE + OWN - 1)
        write(BASE + OWN - 1, BASE + OWN, FACES[1], MEET[1], rx + sx, ry + sy, 1, 0)


def shifts(partner):
    lane = lanes_of((8, 128))
    j = lane + partner
    idx, inside = j & 127, (j >= 0) & (j < 128)

    def before(own, prv, nxt):
        return pltpu.roll(jnp.where(lane == 127, prv, own), 1, 1)

    def after(own, prv, nxt):
        return pltpu.roll(jnp.where(lane == 0, nxt, own), 127, 1)

    def across(own, prv, nxt):
        return jnp.where(inside, pick(own, idx), pick(jnp.where(lane < 64, nxt, prv), idx))

    return before, after, across


def coefficients(m, mt, cv, pv, co):
    rx, ry, sx, sy = (spread(mt, k, m, 8) for k in range(4))
    partner = pv[m : m + 8, :]
    three = [cv[m + s : m + s + 8, :] for s in (0, -1, 1)]
    c = three[0]
    outer = [move(*three) for move in shifts(partner)]
    outer[2] = jnp.where(partner == 0, c, outer[2])
    for k, (gx, gy) in enumerate(((sx, sy), (rx + sx, ry + sy), (rx, ry))):
        length = jnp.sqrt(gx * gx + gy * gy)
        co[k, m : m + 8, :] = outer[k]
        co[3 + k, m : m + 8, :] = length * jnp.sqrt(jnp.maximum(c, outer[k]))
        if k == 2:
            co[6, m : m + 8, :] = gx / length
            co[7, m : m + 8, :] = gy / length


def flux(m, src, pitch, at, mt, cv, pv, co, xt, slot):
    rx, ry, sx, sy = (spread(mt, k, m, 8) for k in range(4))
    c = cv[m : m + 8, :]
    partner = pv[m : m + 8, :]
    wall = partner == 0
    moves = shifts(partner)

    def value(f, n, step=0):
        return spread(src, at(f, n), m + step, pitch)

    def store(f, k, x):
        put(xt, f * 32 + k, slot, XP, x)

    crx, cry, csx, csy = -c * rx, -c * ry, -c * sx, -c * sy
    for n in range(10):
        eta, mx, my = (value(f, n) for f in range(3))
        store(0, n, -(rx * mx + ry * my))
        store(0, 10 + n, -(sx * mx + sy * my))
        store(1, n, crx * eta)
        store(1, 10 + n, csx * eta)
        store(2, n, cry * eta)
        store(2, 10 + n, csy * eta)
    vectors = ((-sx, -sy), (rx + sx, ry + sy), (-rx, -ry))
    for k in range(3):
        gx, gy = vectors[k]
        ce = co[k, m : m + 8, :]
        scale = co[3 + k, m : m + 8, :]
        for j in range(4):
            inner = [value(f, FACES[k][j]) for f in range(3)]
            outer = []
            for f in range(3):
                node = MEET[k][j]
                own = value(f, node)
                prv = value(f, node, -1) if k != 1 else None
                nxt = value(f, node, 1) if k != 0 else None
                outer.append(moves[k](own, prv, nxt))
            if k == 2:
                outer[0] = jnp.where(wall, inner[0], outer[0])
            d_eta, d_mx, d_my = (b - a for a, b in zip(inner, outer))
            if k == 2:
                nx, ny = co[6, m : m + 8, :], co[7, m : m + 8, :]
                twice = -2.0 * (inner[1] * nx + inner[2] * ny)
                d_mx = jnp.where(wall, twice * nx, d_mx)
                d_my = jnp.where(wall, twice * ny, d_my)
            drop = c * inner[0] - ce * outer[0]
            row = 20 + 4 * k + j
            store(0, row, scale * d_eta - gx * d_mx - gy * d_my)
            store(1, row, gx * drop + scale * d_mx)
            store(2, row, gy * drop + scale * d_my)


def product(m, slot, xt, wl, out):
    for pair in range(4):
        parts = []
        for t in (2 * pair, 2 * pair + 1):
            hi, lo = split(xt[(slot + t) * XP : (slot + t + 1) * XP, :])
            parts.append(jnp.concatenate([hi, lo], axis=0))
        both = jnp.concatenate(parts, axis=1)
        res = jnp.dot(wl[:, 0 : 2 * XP], both, preferred_element_type=f32)
        res = res[0:32] + res[32:64]
        tile = m + 2 * pair
        out[tile * RP : (tile + 1) * RP, :] = res[:, 0:128]
        out[(tile + 1) * RP : (tile + 2) * RP, :] = res[:, 128:256]


def weights(diff_ops, lift, wl, tmp, wf):
    wf[...] = jnp.zeros_like(wf)
    base = jnp.zeros((16, 128), f32)
    for i, shift in ((0, 0), (1, 10), (2, 20)):
        tmp[...] = jnp.zeros_like(tmp)
        if i == 2:
            tmp[0:10, 0:12] = 0.5 * lift[...]
        else:
            for n in range(10):
                tmp[n : n + 1, 0:10] = diff_ops[n, i : i + 1, :]
        base = base + (tmp[...] if shift == 0 else pltpu.roll(tmp[...], shift, 1))
    for f in range(3):
        turned = base if f == 0 else pltpu.roll(base, 32 * f, 1)
        wf[f * 10 : f * 10 + 10, :] = turned[0:10]
    w = wf[0:32, :]
    hi = w.astype(bf16).astype(f32)
    low = w - hi
    turned = pltpu.roll(hi, XP, 1)
    lane = lanes_of((32, 128))
    wl[0:32, 0:128] = (hi + jnp.where(lane >= XP, turned, 0.0)).astype(bf16)
    wl[0:32, 128:256] = jnp.where(lane < 64, turned, 0.0).astype(bf16)
    wl[32:64, 0:128] = low.astype(bf16)
    wl[32:64, 128:256] = jnp.zeros((32, 128), bf16)


def child_weights(prolong, pw, tmp, wf):
    for i in range(3):
        wf[...] = jnp.zeros_like(wf)
        tmp[...] = jnp.zeros_like(tmp)
        if i == 0:
            eye = lax.broadcasted_iota(i32, (16, 128), 0) == lanes_of((16, 128))
            tmp[0:10, :] = jnp.where(eye, 1.0, 0.0)[0:10]
        else:
            for n in range(10):
                tmp[n : n + 1, 0:10] = prolong[n, i - 1 : i, :]
        for f in range(3):
            turned = tmp[...] if f == 0 else pltpu.roll(tmp[...], 10 * f, 1)
            wf[pl.ds(f, 10, stride=4), :] = turned[0:10]
        w = wf[...]
        hi = w.astype(bf16).astype(f32)
        low = w - hi
        pw[i * 48 : i * 48 + 48, :] = (hi + pltpu.roll(hi, 32, 1) + pltpu.roll(low, 64, 1)).astype(bf16)


def combine(m, step, qt, r1, r2, st):
    half = 0.5 * step * step
    for f in range(3):
        for n in range(10):
            v = f * 10 + n
            x = spread(qt, state_row(f, n), m, QP) + (step * spread(r1, v, m, RP) + half * spread(r2, v, m, RP))
            put(st, v, m - 16, RP, x)
    put(st, 30, m - 16, RP, jnp.zeros((8, 128), f32))
    put(st, 31, m - 16, RP, jnp.zeros((8, 128), f32))


def place_tables(offset, refine, lr, rr, rv, pk, near, code, lidx, pkw):
    rv[0:8, :] = lr[8:16, :]
    rv[8:40, :] = refine[...]
    rv[40:48, :] = rr[0:8, :]
    bits = rv[...]
    counts = (1 + bits).astype(f32)
    upper = lax.broadcasted_iota(i32, (128, 128), 0) <= lanes_of((128, 128))
    within = jnp.dot(counts.astype(bf16), upper.astype(f32).astype(bf16), preferred_element_type=f32)
    sums = jnp.broadcast_to(within[:, 127:128], (48, 128))
    lower = lanes_of((48, 48)) < lax.broadcasted_iota(i32, (48, 48), 0)
    before = jnp.dot(lower.astype(f32).astype(bf16), sums.astype(bf16), preferred_element_type=f32)
    ends = within + before - before[8:9, :] + offset
    ends = ends.astype(i32)
    pk[0:48, :] = 2 * (ends - 1 - bits) + bits
    pk[48:56, :] = jnp.full((8, 128), 2 * (1 << 20), i32)
    last = jnp.broadcast_to(ends[:, 127:128], (48, 128))
    reached = (last <= lanes_of((48, 128)) * 128).astype(f32)
    first = jnp.sum(reached, axis=0, keepdims=True).astype(i32)
    near[...] = jnp.broadcast_to(first, (8, 128))
    tiles = [near[0, r] for r in range(48)]
    for r in range(48):
        pkw[0, r : r + 1, :] = pk[pl.ds(tiles[r], 1), :]
        pkw[1, r : r + 1, :] = pk[pl.ds(tiles[r] + 1, 1), :]
    for g in range(6):
        rows = slice(8 * g, 8 * g + 8)
        p0, p1 = pkw[0, rows, :], pkw[1, rows, :]
        e0 = (p0 >> 1) + 1 + (p0 & 1)
        e1 = (p1 >> 1) + 1 + (p1 & 1)
        slot = (8 * g + lax.broadcasted_iota(i32, (8, 128), 0)) * 128 + lanes_of((8, 128))
        over = jnp.broadcast_to(e0[:, 127:128], (8, 128)) <= slot
        pos = jnp.zeros((8, 128), i32)
        for s in (64, 32, 16, 8, 4, 2, 1):
            probe = pos + (s - 1)
            e = jnp.where(over, pick(e1, probe), pick(e0, probe))
            pos = jnp.where(e <= slot, pos + s, pos)
        got = jnp.where(over, pick(p1, pos), pick(p0, pos))
        which = slot - (got >> 1)
        lidx[rows, :] = jnp.where(over, pos + 128, pos)
        code[rows, :] = jnp.where((got & 1) == 0, 0, 1 + which)
    return tiles


def place(tiles, st, pw, lidx, code, out):
    for pair in range(24):
        parts = []
        for r in (2 * pair, 2 * pair + 1):
            begin = pl.multiple_of(tiles[r] * RP, RP)
            near = st[pl.ds(begin, RP), :]
            far = st[pl.ds(pl.multiple_of(begin + RP, RP), RP), :]
            idx = jnp.broadcast_to(lidx[r : r + 1, :], (RP, 128))
            low = idx & 127
            s = jnp.where(idx < 128, pick(near, low), pick(far, low))
            hi, lo = split(s)
            parts.append(jnp.concatenate([hi, lo, hi], axis=0))
        res = jnp.dot(pw[:, 0:96], jnp.concatenate(parts, axis=1), preferred_element_type=f32)
        for i in range(2):
            r = 2 * pair + i
            one = res[:, 128 * i : 128 * i + 128]
            kind = jnp.broadcast_to(code[r : r + 1, :], (48, 128))
            new = jnp.where(kind == 0, one[0:48], jnp.where(kind == 1, one[48:96], one[96:144]))
            for n in range(10):
                out[n, :, r * 128 : (r + 1) * 128] = new[4 * n : 4 * n + 3]


def local(
    total, cols,
    state, metric, depth, partner, refine, diff_ops, lift, prolong,
    ls, lm, ld, lp, lr, rs, rm, rd, rp, rr, stat,
    out,
    qt, mt, cv, pv, co, xt, r1, r2, st, wl, pw, tmp, wf, rv, pk, near, code, lidx, pkw,
):
    me = lax.axis_index("row") * cols + lax.axis_index("col")
    ends = (me == 0, me == total - 1)
    weights(diff_ops, lift, wl, tmp, wf)
    child_weights(prolong, pw, tmp, wf)
    load_tiles((state, metric, depth, partner), (ls, lm, ld, lp), (rs, rm, rd, rp), qt, mt, cv, pv, ends)
    mirror(qt, QP, state_row, mt, ends)
    for g in range(7):
        m = 8 + 8 * g
        coefficients(m, mt, cv, pv, co)
        flux(m, qt, QP, state_row, mt, cv, pv, co, xt, 8 * (g % 2))
        product(m, 8 * (g % 2), xt, wl, r1)
    r1[64 * RP : 65 * RP, :] = r1[8 * RP : 9 * RP, :]
    mirror(r1, RP, result_row, mt, ends)
    step = COURANT / stat[0:1, :]
    for g in range(1, 7):
        m = 8 + 8 * g
        flux(m, r1, RP, result_row, mt, cv, pv, co, xt, 8 * (g % 2))
        product(m, 8 * (g % 2), xt, wl, r2)
        combine(m, step, qt, r1, r2, st)
    tiles = place_tables(stat[1:2, :], refine, lr, rr, rv, pk, near, code, lidx, pkw)
    place(tiles, st, pw, lidx, code, out)


def solution(mesh):
    rows, cols = mesh.shape["row"], mesh.shape["col"]
    total = rows * cols
    low = 16 if total % 256 == 0 else max(total // 2, 1)
    high = total // low

    def shards(state, depth, metric, partner, refine, diff_ops, lift, prolong):
        depth, partner, refine = (a.reshape(OWN, 128) for a in (depth, partner, refine))
        state, diff_ops, prolong = (a.transpose(1, 0, 2) for a in (state, diff_ops, prolong))
        vm = pl.BlockSpec(memory_space=pltpu.VMEM)
        side = [
            jax.ShapeDtypeStruct((10, 3, WIDE), f32),
            jax.ShapeDtypeStruct((4, WIDE), f32),
            jax.ShapeDtypeStruct((16, 128), f32),
            jax.ShapeDtypeStruct((16, 128), i32),
            jax.ShapeDtypeStruct((16, 128), i32),
        ]
        got = pl.pallas_call(
            functools.partial(exchange, rows, cols, low),
            out_shape=side + side + [jax.ShapeDtypeStruct((8, 128), f32)],
            in_specs=[vm] * 5,
            out_specs=[vm] * 11,
            scratch_shapes=[
                pltpu.VMEM((OWN * 8, 128), f32),
                pltpu.VMEM((8, 128), f32),
                pltpu.VMEM((low - 1, 8, 128), f32),
                pltpu.VMEM((8, 128), f32),
                pltpu.VMEM((high - 1, 8, 128), f32),
                pltpu.SemaphoreType.DMA((10,)),
                pltpu.SemaphoreType.DMA((10,)),
                pltpu.SemaphoreType.DMA((low - 1,)),
                pltpu.SemaphoreType.DMA((low - 1,)),
                pltpu.SemaphoreType.DMA((high - 1,)),
                pltpu.SemaphoreType.DMA((high - 1,)),
            ],
            compiler_params=pltpu.CompilerParams(collective_id=0, has_side_effects=True),
            name="exchange",
        )(state, metric, depth, partner, refine)
        new = pl.pallas_call(
            functools.partial(local, total, cols),
            out_shape=jax.ShapeDtypeStruct((10, 3, OWN * 192), f32),
            in_specs=[vm] * 19,
            out_specs=vm,
            scratch_shapes=[
                pltpu.VMEM((MEM * QP, 128), f32),
                pltpu.VMEM((MEM * 8, 128), f32),
                pltpu.VMEM((MEM, 128), f32),
                pltpu.VMEM((MEM, 128), i32),
                pltpu.VMEM((8, MEM, 128), f32),
                pltpu.VMEM((16 * XP, 128), f32),
                pltpu.VMEM((MEM * RP, 128), f32),
                pltpu.VMEM((MEM * RP, 128), f32),
                pltpu.VMEM((49 * RP, 128), f32),
                pltpu.VMEM((64, 256), bf16),
                pltpu.VMEM((144, 128), bf16),
                pltpu.VMEM((16, 128), f32),
                pltpu.VMEM((48, 128), f32),
                pltpu.VMEM((48, 128), i32),
                pltpu.VMEM((56, 128), i32),
                pltpu.VMEM((8, 128), i32),
                pltpu.VMEM((48, 128), i32),
                pltpu.VMEM((48, 128), i32),
                pltpu.VMEM((2, 48, 128), i32),
            ],
            name="local",
        )(state, metric, depth, partner, refine, diff_ops, lift, prolong, *got)
        return new.transpose(1, 0, 2)

    halves = ("row", "col")
    return jax.shard_map(
        shards,
        mesh=mesh,
        in_specs=(P(None, None, halves), P(halves), P(None, halves), P(halves), P(halves), P(), P(), P()),
        out_specs=P(None, None, halves),
        check_vma=False,
    )
```

time: 1170 us -> 37.3 us (0.03)
  the two profiles are of different devices: /device:TPU:2 before, /device:TPU:1 now
where the time goes in v1:
time: 37.3 us; the launch traced here: 37.2 us
  Pallas kernels  37.2 us (100%)
    pallas_call x1, Pallas kernels, shards(): pl.pallas_call(functools.partial(exchange, rows, cols, low), out_shape=si...  23.8 us
    pallas_call x1, Pallas kernels, shards(): pl.pallas_call(functools.partial(local, total, cols), out_shape=jax.Shape...  13.4 us

profile of v1, /device:TPU:1, one launch (start us, length us, event | category | flops | bytes accessed | tf_op | source)
XLA Modules:
  0.0 37.2 jit_solution(9443754397746573872)
XLA Ops:
  0.0 23.8 %exchange.1 = (f32[10,3,1152]{2,1,0:T(4,128)}, f32[4,1152]{1,0:T(4,128)}, f32[16,128]{1,0:T(8,128)}, s32[16,128]{1,0:T(8,128)}, s32[16,128]{1,0:T(8,128)}, /*ind...) custom-call(f32[10,3,4096]{2,1,0:T(4,128)} %bitcast.7, ...), custom_call_target="tpu_custom_call" | custom-call | tf_op jit(solution)/shard_map/exchange/pallas_call | solution.py:488
  23.8 13.4 %local.1 = f32[10,3,6144]{2,1,0:T(4,128)} custom-call(f32[10,3,4096]{2,1,0:T(4,128)} %bitcast.8, f32[4,4096]{1,0:T(4,128)} %metric.3, f32[32,128]{1,0:T(8,128)} %bitcast.10, s32[32,128]{1,0:T(8,128)} %bitcast.12, s32[32,128]{1,0:T(8,128)} %bitcast.14, f32[10,2,10]{2,1,0:T(2,128)} %bitcast.15, f32[10,12]{1,0:T(8,128)} %lift.1, f32[10,2,10]{2,1,0:T(2,128)} %bitcast.16, ...), custom_call_target="tpu_custom_call" | custom-call | tf_op jit(solution)/shard_map/local/pallas_call | solution.py:509

commit v2 on v1

--- a/solution.py
+++ b/solution.py
@@ -16,9 +16,12 @@
 WIDE = HALO * 128
 BASE = 24
 MEM = 72
-QP = 40
-RP = 32
+QP = 41
+RR = 32
+RP = 33
+MP = 9
 XP = 96
+XS = 97
 
 FACES = ((0, 1, 2, 3), (3, 6, 8, 9), (9, 7, 4, 0))
 MEET = ((9, 8, 6, 3), (3, 2, 1, 0), (0, 4, 7, 9))
@@ -57,11 +60,24 @@
     return hi, (x - hi.astype(f32)).astype(bf16)
 
 
-def exchange(
+def joined(own, box, size, position):
+    part = box[0 : size - 1, :]
+    member = lax.broadcasted_iota(i32, part.shape, 0) + 1
+    best = jnp.maximum(own, jnp.max(part, axis=0, keepdims=True))
+    both = own + jnp.sum(part, axis=0, keepdims=True)
+    before = jnp.sum(jnp.where(member <= position, part, 0.0), axis=0, keepdims=True)
+    return jnp.where(lanes_of((1, 128)) < 64, best, both), before
+
+
+def advance(
     rows, cols, low,
-    state, metric, depth, partner, refine,
-    ls, lm, ld, lp, lr, rs, rm, rd, rp, rr, stat,
-    mt, mine, box1, pair2, box2, send, recv, send1, recv1, send2, recv2,
+    state, metric, depth, partner, refine, diff_ops, lift, prolong,
+    st, pk, pw, stat,
+    sv, gv, dv, av, bv, wd, wt, wc,
+    ls, lm, ld, lp, lr, rs, rm, rd, rp, rr,
+    qt, mt, cv, pv, co, xt, r1, r2, wl, tmp, wf, rv,
+    mine, box1, mine2, box2,
+    here, send, recv, send1, recv1, send2, recv2,
 ):
     total = rows * cols
     high = total // low
@@ -81,64 +97,100 @@
     for peer in everyone:
         pl.semaphore_signal(barrier, inc=1, device_id=peer, device_id_type=MESH)
 
+    pairs = (
+        (metric, gv), (depth, dv), (refine, bv), (state, sv), (partner, av), (diff_ops, wd), (lift, wt), (prolong, wc))
+    loads = [pltpu.make_async_copy(a, b, here.at[k]) for k, (a, b) in enumerate(pairs)]
+    for load in loads:
+        load.start()
+    for load in loads[:3]:
+        load.wait()
     for t in range(OWN):
-        mt[t * 8 : t * 8 + 4, :] = metric[:, t * 128 : (t + 1) * 128]
-    grads = [mt[pl.ds(k, OWN, stride=8), :] for k in range(4)]
-    rate = wave_rate(depth[...], grads)
-    top = jnp.max(jnp.max(rate, axis=1, keepdims=True), axis=0, keepdims=True)
-    count = refine[...].astype(f32)
-    count = jnp.sum(jnp.sum(count, axis=1, keepdims=True), axis=0, keepdims=True)
-    first_row = lax.broadcasted_iota(i32, (8, 128), 0) == 0
-    mine[...] = jnp.where(first_row, top, count)
-
-    pl.semaphore_wait(barrier, len(everyone))
-
+        lay_metric(mt, BASE + t, gv, t)
+    grads = [mt[pl.ds(BASE * MP + k, OWN, stride=MP), :] for k in range(4)]
+    rate = wave_rate(dv[...], grads)
+    top = jnp.max(jnp.max(rate, axis=0, keepdims=True), axis=1, keepdims=True)
+    count = jnp.sum(bv[...].astype(f32), axis=0, keepdims=True)
+    count = jnp.sum(count, axis=1, keepdims=True)
+    half = lanes_of((1, 128)) < 64
+    own = jnp.where(half, top, count)
+    mine[0:1, :] = own
+
+    def round_of(source, box, peers, sems, rems):
+        return [
+            pltpu.make_async_remote_copy(
+                src_ref=source.at[pl.ds(0, 1)], dst_ref=box.at[pl.ds(d, 1)], send_sem=sems.at[d], recv_sem=rems.at[d],
+                device_id=peer, device_id_type=MESH)
+            for d, peer in enumerate(peers)
+        ]
+
+    round1 = round_of(mine, box1, peers1, send1, recv1)
+    round2 = round_of(mine2, box2, peers2, send2, recv2)
+    tail, head = pl.ds((OWN - HALO) * 128, WIDE), pl.ds(0, WIDE)
     copies = []
-    sides = (
-        (right, (state.at[:, :, pl.ds((OWN - HALO) * 128, WIDE)], metric.at[:, pl.ds((OWN - HALO) * 128, WIDE)],
-                 depth.at[pl.ds(16, 16)], partner.at[pl.ds(16, 16)], refine.at[pl.ds(16, 16)]), (ls, lm, ld, lp, lr)),
-        (left, (state.at[:, :, pl.ds(0, WIDE)], metric.at[:, pl.ds(0, WIDE)],
-                depth.at[pl.ds(0, 16)], partner.at[pl.ds(0, 16)], refine.at[pl.ds(0, 16)]), (rs, rm, rd, rp, rr)),
-    )
-    for peer, sources, targets in sides:
+    for peer, wide, short, targets in (
+        (right, tail, pl.ds(16, 16), (ls, lm, ld, lp, lr)),
+        (left, head, pl.ds(0, 16), (rs, rm, rd, rp, rr)),
+    ):
+        sources = (state.at[:, :, wide], metric.at[:, wide], depth.at[short], partner.at[short], refine.at[short])
         for source, target in zip(sources, targets):
             k = len(copies)
             copies.append(pltpu.make_async_remote_copy(
                 src_ref=source, dst_ref=target, send_sem=send.at[k], recv_sem=recv.at[k],
                 device_id=peer, device_id_type=MESH))
+
+    pl.semaphore_wait(barrier, len(everyone))
+    for copy in round1 + copies:
+        copy.start()
+
+    for load in loads[3:]:
+        load.wait()
+    ends = (me == 0, me == total - 1)
+    weights(wd, wt, wl, tmp, wf)
+    for t in range(OWN):
+        lay_state(qt, BASE + t, sv, t)
+    cv[BASE : BASE + OWN, :] = GRAVITY * dv[...]
+    pv[BASE : BASE + OWN, :] = av[...]
+
+    def first_rate(g):
+        m = 8 + 8 * g
+        coefficients(m, mt, cv, pv, co)
+        flux(m, qt, QP, state_row, mt, cv, pv, co, xt, 8 * (g % 2))
+        product(m, 8 * (g % 2), xt, wl, r1)
+
+    for g in (3, 4):
+        first_rate(g)
+    child_weights(wc, pw, tmp, wf)
     for copy in copies:
+        copy.wait_recv()
+    load_rims((ls, lm, ld, lp), (rs, rm, rd, rp), qt, mt, cv, pv, ends)
+    mirror(qt, QP, state_row, mt, ends)
+    for g in (2, 5, 6, 1, 0):
+        first_rate(g)
+    for copy in round1:
+        copy.wait_recv()
+    own, before1 = joined(own, box1, low, lo)
+    mine2[0:1, :] = own
+    for copy in round2:
         copy.start()
-
-    def round_of(source, box, peers, sems, rems):
-        batch = [
-            pltpu.make_async_remote_copy(
-                src_ref=source, dst_ref=box.at[d], send_sem=sems.at[d], recv_sem=rems.at[d],
-                device_id=peer, device_id_type=MESH)
-            for d, peer in enumerate(peers)
-        ]
-        for copy in batch:
-            copy.start()
-        for copy in batch:
-            copy.wait()
-
-    def joined(own, box, size, position):
-        best, both, before = own, own, jnp.zeros_like(own)
-        for d in range(size - 1):
-            part = box[d]
-            best = jnp.maximum(best, part)
-            both = both + part
-            before = before + jnp.where(d + 1 <= position, part, 0.0)
-        return best, both, before
-
-    round_of(mine, box1, peers1, send1, recv1)
-    best, both, before1 = joined(mine[...], box1, low, lo)
-    pair2[...] = jnp.where(first_row, best, both)
-    round_of(pair2, box2, peers2, send2, recv2)
-    best, _, before2 = joined(pair2[...], box2, high, hi)
-    offset = before1 + before2 - (me * (OWN * 64)).astype(f32)
-    stat[...] = jnp.where(first_row, best, offset)
-    for copy in copies:
-        copy.wait()
+    r1[64 * RP : 65 * RP, :] = r1[8 * RP : 9 * RP, :]
+    mirror(r1, RP, result_row, mt, ends)
+    for g in range(1, 7):
+        m = 8 + 8 * g
+        flux(m, r1, RP, result_row, mt, cv, pv, co, xt, 8 * (g % 2))
+        product(m, 8 * (g % 2), xt, wl, r2)
+    prefix(lr, bv, rr, rv, pk)
+    for copy in round2:
+        copy.wait_recv()
+    own, before2 = joined(own, box2, high, hi)
+    best = jnp.where(half, own, pltpu.roll(own, 64, 1))
+    before = before1 + before2
+    before = jnp.where(half, pltpu.roll(before, 64, 1), before)
+    stat[0:1, :] = before - (me * (OWN * 64)).astype(f32)
+    step = COURANT / best
+    for g in range(1, 7):
+        combine(8 + 8 * g, step, qt, r1, r2, st)
+    for copy in round1 + round2 + copies:
+        copy.wait_send()
 
 
 def wave_rate(depth, grads):
@@ -147,19 +199,23 @@
     return jnp.sqrt(GRAVITY * depth) * jnp.maximum(jnp.maximum(lengths[0], lengths[1]), lengths[2])
 
 
-def load_tiles(own, left, right, qt, mt, cv, pv, ends):
-    state, metric, depth, partner = own
+def lay_state(qt, m, s, t):
+    for n in range(10):
+        qt[m * QP + 4 * n : m * QP + 4 * n + 3, :] = s[n, :, t * 128 : (t + 1) * 128]
+
+
+def lay_metric(mt, m, g, t):
+    mt[m * MP : m * MP + 4, :] = g[:, t * 128 : (t + 1) * 128]
+
+
+def load_rims(left, right, qt, mt, cv, pv, ends):
     ls, lm, ld, lp = left
     rs, rm, rd, rp = right
 
     def lay(m, s, g, t):
-        here = slice(t * 128, (t + 1) * 128)
-        for n in range(10):
-            qt[m * QP + 4 * n : m * QP + 4 * n + 3, :] = s[n, :, here]
-        mt[m * 8 : m * 8 + 4, :] = g[:, here]
-
-    for t in range(OWN):
-        lay(BASE + t, state, metric, t)
+        lay_state(qt, m, s, t)
+        lay_metric(mt, m, g, t)
+
     for t in range(HALO):
         lay(BASE - HALO + t, ls, lm, t)
         if t < HALO - 1:
@@ -167,13 +223,12 @@
     lay(8, rs, rm, HALO - 1)
     lay(64, rs, rm, HALO - 1)
     lay(7, rs, rm, HALO - 2)
-    for into, mid, before, after in ((cv, depth, ld, rd), (pv, partner, lp, rp)):
-        into[BASE : BASE + OWN, :] = mid[...]
-        into[BASE - HALO : BASE, :] = before[16 - HALO : 16, :]
-        into[BASE + OWN : BASE + OWN + 8, :] = after[0:8, :]
-        into[7:8, :] = after[7:8, :]
-        into[8:9, :] = after[8:9, :]
-        into[64:65, :] = after[8:9, :]
+    for into, before, after, scale in ((cv, ld, rd, GRAVITY), (pv, lp, rp, 1)):
+        into[BASE - HALO : BASE, :] = scale * before[16 - HALO : 16, :]
+        into[BASE + OWN : BASE + OWN + 8, :] = scale * after[0:8, :]
+        into[7:8, :] = scale * after[7:8, :]
+        into[8:9, :] = scale * after[8:9, :]
+        into[64:65, :] = scale * after[8:9, :]
     first, last = ends
 
     @pl.when(first)
@@ -184,8 +239,6 @@
     def _():
         cv[BASE + OWN : BASE + OWN + 1, :] = pltpu.roll(cv[BASE + OWN - 1 : BASE + OWN, :], 1, 1)
 
-    cv[...] = GRAVITY * cv[...]
-
 
 def mirror(src, pitch, at, mt, ends):
     lane = lanes_of((1, 128))
@@ -194,7 +247,7 @@
         return src[tile * pitch + v : tile * pitch + v + 1, :]
 
     def grads(tile):
-        return [mt[tile * 8 + k : tile * 8 + k + 1, :] for k in range(4)]
+        return [mt[tile * MP + k : tile * MP + k + 1, :] for k in range(4)]
 
     def write(tile, rim, nodes, meet, gx, gy, shift, target):
         length = jnp.sqrt(gx * gx + gy * gy)
@@ -239,7 +292,7 @@
 
 
 def coefficients(m, mt, cv, pv, co):
-    rx, ry, sx, sy = (spread(mt, k, m, 8) for k in range(4))
+    rx, ry, sx, sy = (spread(mt, k, m, MP) for k in range(4))
     partner = pv[m : m + 8, :]
     three = [cv[m + s : m + s + 8, :] for s in (0, -1, 1)]
     c = three[0]
@@ -255,7 +308,7 @@
 
 
 def flux(m, src, pitch, at, mt, cv, pv, co, xt, slot):
-    rx, ry, sx, sy = (spread(mt, k, m, 8) for k in range(4))
+    rx, ry, sx, sy = (spread(mt, k, m, MP) for k in range(4))
     c = cv[m : m + 8, :]
     partner = pv[m : m + 8, :]
     wall = partner == 0
@@ -265,7 +318,7 @@
         return spread(src, at(f, n), m + step, pitch)
 
     def store(f, k, x):
-        put(xt, f * 32 + k, slot, XP, x)
+        put(xt, f * 32 + k, slot, XS, x)
 
     crx, cry, csx, csy = -c * rx, -c * ry, -c * sx, -c * sy
     for n in range(10):
@@ -309,14 +362,14 @@
     for pair in range(4):
         parts = []
         for t in (2 * pair, 2 * pair + 1):
-            hi, lo = split(xt[(slot + t) * XP : (slot + t + 1) * XP, :])
+            hi, lo = split(xt[(slot + t) * XS : (slot + t) * XS + XP, :])
             parts.append(jnp.concatenate([hi, lo], axis=0))
         both = jnp.concatenate(parts, axis=1)
         res = jnp.dot(wl[:, 0 : 2 * XP], both, preferred_element_type=f32)
         res = res[0:32] + res[32:64]
         tile = m + 2 * pair
-        out[tile * RP : (tile + 1) * RP, :] = res[:, 0:128]
-        out[(tile + 1) * RP : (tile + 2) * RP, :] = res[:, 128:256]
+        out[tile * RP : tile * RP + RR, :] = res[:, 0:128]
+        out[(tile + 1) * RP : (tile + 1) * RP + RR, :] = res[:, 128:256]
 
 
 def weights(diff_ops, lift, wl, tmp, wf):
@@ -374,7 +427,7 @@
     put(st, 31, m - 16, RP, jnp.zeros((8, 128), f32))
 
 
-def place_tables(offset, refine, lr, rr, rv, pk, near, code, lidx, pkw):
+def prefix(lr, refine, rr, rv, pk):
     rv[0:8, :] = lr[8:16, :]
     rv[8:40, :] = refine[...]
     rv[40:48, :] = rr[0:8, :]
@@ -385,10 +438,14 @@
     sums = jnp.broadcast_to(within[:, 127:128], (48, 128))
     lower = lanes_of((48, 48)) < lax.broadcasted_iota(i32, (48, 48), 0)
     before = jnp.dot(lower.astype(f32).astype(bf16), sums.astype(bf16), preferred_element_type=f32)
-    ends = within + before - before[8:9, :] + offset
-    ends = ends.astype(i32)
+    ends = (within + before - before[8:9, :]).astype(i32)
     pk[0:48, :] = 2 * (ends - 1 - bits) + bits
-    pk[48:56, :] = jnp.full((8, 128), 2 * (1 << 20), i32)
+    pk[48:56, :] = jnp.full((8, 128), 1 << 21, i32)
+
+
+def tables(offset, rel, pk, near, code, lidx, pkw):
+    pk[...] = rel[...] + 2 * offset.astype(i32)
+    ends = (pk[0:48, :] >> 1) + 1 + (pk[0:48, :] & 1)
     last = jnp.broadcast_to(ends[:, 127:128], (48, 128))
     reached = (last <= lanes_of((48, 128)) * 128).astype(f32)
     first = jnp.sum(reached, axis=0, keepdims=True).astype(i32)
@@ -416,56 +473,39 @@
     return tiles
 
 
-def place(tiles, st, pw, lidx, code, out):
+def place(rel, pw, stat, st_in, out, st, new_tiles, pk, near, code, lidx, pkw, sems):
+    load = pltpu.make_async_copy(st_in, st, sems.at[0])
+    load.start()
+    tiles = tables(stat[0:1, :], rel, pk, near, code, lidx, pkw)
+    load.wait()
+    weight = pw[:, 0:96]
+    stores = []
     for pair in range(24):
         parts = []
         for r in (2 * pair, 2 * pair + 1):
-            begin = pl.multiple_of(tiles[r] * RP, RP)
-            near = st[pl.ds(begin, RP), :]
-            far = st[pl.ds(pl.multiple_of(begin + RP, RP), RP), :]
-            idx = jnp.broadcast_to(lidx[r : r + 1, :], (RP, 128))
+            begin = tiles[r] * RP
+            near_tile = st[pl.ds(begin, RR), :]
+            far_tile = st[pl.ds(begin + RP, RR), :]
+            idx = jnp.broadcast_to(lidx[r : r + 1, :], (RR, 128))
             low = idx & 127
-            s = jnp.where(idx < 128, pick(near, low), pick(far, low))
+            s = jnp.where(idx < 128, pick(near_tile, low), pick(far_tile, low))
             hi, lo = split(s)
             parts.append(jnp.concatenate([hi, lo, hi], axis=0))
-        res = jnp.dot(pw[:, 0:96], jnp.concatenate(parts, axis=1), preferred_element_type=f32)
+        res = jnp.dot(weight, jnp.concatenate(parts, axis=1), preferred_element_type=f32)
         for i in range(2):
             r = 2 * pair + i
             one = res[:, 128 * i : 128 * i + 128]
             kind = jnp.broadcast_to(code[r : r + 1, :], (48, 128))
             new = jnp.where(kind == 0, one[0:48], jnp.where(kind == 1, one[48:96], one[96:144]))
             for n in range(10):
-                out[n, :, r * 128 : (r + 1) * 128] = new[4 * n : 4 * n + 3]
-
-
-def local(
-    total, cols,
-    state, metric, depth, partner, refine, diff_ops, lift, prolong,
-    ls, lm, ld, lp, lr, rs, rm, rd, rp, rr, stat,
-    out,
-    qt, mt, cv, pv, co, xt, r1, r2, st, wl, pw, tmp, wf, rv, pk, near, code, lidx, pkw,
-):
-    me = lax.axis_index("row") * cols + lax.axis_index("col")
-    ends = (me == 0, me == total - 1)
-    weights(diff_ops, lift, wl, tmp, wf)
-    child_weights(prolong, pw, tmp, wf)
-    load_tiles((state, metric, depth, partner), (ls, lm, ld, lp), (rs, rm, rd, rp), qt, mt, cv, pv, ends)
-    mirror(qt, QP, state_row, mt, ends)
-    for g in range(7):
-        m = 8 + 8 * g
-        coefficients(m, mt, cv, pv, co)
-        flux(m, qt, QP, state_row, mt, cv, pv, co, xt, 8 * (g % 2))
-        product(m, 8 * (g % 2), xt, wl, r1)
-    r1[64 * RP : 65 * RP, :] = r1[8 * RP : 9 * RP, :]
-    mirror(r1, RP, result_row, mt, ends)
-    step = COURANT / stat[0:1, :]
-    for g in range(1, 7):
-        m = 8 + 8 * g
-        flux(m, r1, RP, result_row, mt, cv, pv, co, xt, 8 * (g % 2))
-        product(m, 8 * (g % 2), xt, wl, r2)
-        combine(m, step, qt, r1, r2, st)
-    tiles = place_tables(stat[1:2, :], refine, lr, rr, rv, pk, near, code, lidx, pkw)
-    place(tiles, st, pw, lidx, code, out)
+                new_tiles[n, :, r * 128 : (r + 1) * 128] = new[4 * n : 4 * n + 3]
+        if pair % 6 == 5:
+            part = pl.ds((pair // 6) * 1536, 1536)
+            store = pltpu.make_async_copy(new_tiles.at[:, :, part], out.at[:, :, part], sems.at[1 + pair // 6])
+            store.start()
+            stores.append(store)
+    for store in stores:
+        store.wait()
 
 
 def solution(mesh):
@@ -473,29 +513,51 @@
     total = rows * cols
     low = 16 if total % 256 == 0 else max(total // 2, 1)
     high = total // low
+    placed = OWN + OWN // 2
 
     def shards(state, depth, metric, partner, refine, diff_ops, lift, prolong):
         depth, partner, refine = (a.reshape(OWN, 128) for a in (depth, partner, refine))
         state, diff_ops, prolong = (a.transpose(1, 0, 2) for a in (state, diff_ops, prolong))
-        vm = pl.BlockSpec(memory_space=pltpu.VMEM)
+        args = (state, metric, depth, partner, refine, diff_ops, lift, prolong)
+        vm, hbm = pl.BlockSpec(memory_space=pltpu.VMEM), pl.BlockSpec(memory_space=pl.ANY)
         side = [
-            jax.ShapeDtypeStruct((10, 3, WIDE), f32),
-            jax.ShapeDtypeStruct((4, WIDE), f32),
-            jax.ShapeDtypeStruct((16, 128), f32),
-            jax.ShapeDtypeStruct((16, 128), i32),
-            jax.ShapeDtypeStruct((16, 128), i32),
+            pltpu.VMEM((10, 3, WIDE), f32),
+            pltpu.VMEM((4, WIDE), f32),
+            pltpu.VMEM((16, 128), f32),
+            pltpu.VMEM((16, 128), i32),
+            pltpu.VMEM((16, 128), i32),
         ]
-        got = pl.pallas_call(
-            functools.partial(exchange, rows, cols, low),
-            out_shape=side + side + [jax.ShapeDtypeStruct((8, 128), f32)],
-            in_specs=[vm] * 5,
-            out_specs=[vm] * 11,
-            scratch_shapes=[
-                pltpu.VMEM((OWN * 8, 128), f32),
+        st, pk, pw, stat = pl.pallas_call(
+            functools.partial(advance, rows, cols, low),
+            out_shape=[
+                jax.ShapeDtypeStruct((((placed + 1) * RP + 7) // 8 * 8, 128), f32),
+                jax.ShapeDtypeStruct((56, 128), i32),
+                jax.ShapeDtypeStruct((144, 128), bf16),
+                jax.ShapeDtypeStruct((8, 128), f32),
+            ],
+            in_specs=[hbm] * 8,
+            out_specs=[vm] * 4,
+            scratch_shapes=[pltpu.VMEM(a.shape, a.dtype) for a in args]
+            + side
+            + side
+            + [
+                pltpu.VMEM((MEM * QP, 128), f32),
+                pltpu.VMEM((MEM * MP, 128), f32),
+                pltpu.VMEM((MEM, 128), f32),
+                pltpu.VMEM((MEM, 128), i32),
+                pltpu.VMEM((8, MEM, 128), f32),
+                pltpu.VMEM((16 * XS, 128), f32),
+                pltpu.VMEM((MEM * RP, 128), f32),
+                pltpu.VMEM((MEM * RP, 128), f32),
+                pltpu.VMEM((64, 256), bf16),
+                pltpu.VMEM((16, 128), f32),
+                pltpu.VMEM((48, 128), f32),
+                pltpu.VMEM((48, 128), i32),
                 pltpu.VMEM((8, 128), f32),
-                pltpu.VMEM((low - 1, 8, 128), f32),
+                pltpu.VMEM((low, 128), f32),
                 pltpu.VMEM((8, 128), f32),
-                pltpu.VMEM((high - 1, 8, 128), f32),
+                pltpu.VMEM((high, 128), f32),
+                pltpu.SemaphoreType.DMA((8,)),
                 pltpu.SemaphoreType.DMA((10,)),
                 pltpu.SemaphoreType.DMA((10,)),
                 pltpu.SemaphoreType.DMA((low - 1,)),
@@ -504,36 +566,25 @@
                 pltpu.SemaphoreType.DMA((high - 1,)),
             ],
             compiler_params=pltpu.CompilerParams(collective_id=0, has_side_effects=True),
-            name="exchange",
-        )(state, metric, depth, partner, refine)
+            name="advance",
+        )(*args)
         new = pl.pallas_call(
-            functools.partial(local, total, cols),
-            out_shape=jax.ShapeDtypeStruct((10, 3, OWN * 192), f32),
-            in_specs=[vm] * 19,
-            out_specs=vm,
+            place,
+            out_shape=jax.ShapeDtypeStruct((10, 3, placed * 128), f32),
+            in_specs=[vm] * 3 + [hbm],
+            out_specs=hbm,
             scratch_shapes=[
-                pltpu.VMEM((MEM * QP, 128), f32),
-                pltpu.VMEM((MEM * 8, 128), f32),
-                pltpu.VMEM((MEM, 128), f32),
-                pltpu.VMEM((MEM, 128), i32),
-                pltpu.VMEM((8, MEM, 128), f32),
-                pltpu.VMEM((16 * XP, 128), f32),
-                pltpu.VMEM((MEM * RP, 128), f32),
-                pltpu.VMEM((MEM * RP, 128), f32),
-                pltpu.VMEM((49 * RP, 128), f32),
-                pltpu.VMEM((64, 256), bf16),
-                pltpu.VMEM((144, 128), bf16),
-                pltpu.VMEM((16, 128), f32),
-                pltpu.VMEM((48, 128), f32),
-                pltpu.VMEM((48, 128), i32),
+                pltpu.VMEM(st.shape, f32),
+                pltpu.VMEM((10, 3, placed * 128), f32),
                 pltpu.VMEM((56, 128), i32),
                 pltpu.VMEM((8, 128), i32),
                 pltpu.VMEM((48, 128), i32),
                 pltpu.VMEM((48, 128), i32),
                 pltpu.VMEM((2, 48, 128), i32),
+                pltpu.SemaphoreType.DMA((5,)),
             ],
-            name="local",
-        )(state, metric, depth, partner, refine, diff_ops, lift, prolong, *got)
+            name="place",
+        )(pk, pw, stat, st)
         return new.transpose(1, 0, 2)
 
     halves = ("row", "col")

time: 37.3 us -> 26.9 us (0.72)
  Pallas kernels: 37.2 us -> 26.7 us
    pallas_call x2, Pallas kernels: 37.2 us -> 26.7 us  [the longest x1 22.8 us: shards(): pl.pallas_call(functools.partial(advance, rows, cols, low), out_shape=[ja...]
where the time goes in v2:
time: 26.9 us; the launch traced here: 26.7 us
  Pallas kernels  26.7 us (99%)
    pallas_call x1, Pallas kernels, shards(): pl.pallas_call(functools.partial(advance, rows, cols, low), out_shape=[ja...  22.8 us
    pallas_call x1, Pallas kernels, shards(): pl.pallas_call(place, out_shape=jax.ShapeDtypeStruct((10, 3, placed * 128...  3.91 us

profile of v2, /device:TPU:1, one launch (start us, length us, event | category | flops | bytes accessed | tf_op | source)
XLA Modules:
  0.0 26.7 jit_solution(14746465506451788760)
XLA Ops:
  0.0 22.8 %advance.1 = (f32[1624,128]{1,0:T(8,128)}, s32[56,128]{1,0:T(8,128)}, bf16[144,128]{1,0:T(8,128)(2,1)}, f32[8,128]{1,0:T(8,128)}) custom-call(f32[10,3,4096]{2,1,0:T(4,128)} %bitcast.7, f32[4,4096]{1,0:T(4,128)} %metric.1, f32[32,128]{1,0:T(8,128)} %bitcast.8, s32[32,128]{1,0:T(8,128)} %bitcast.9, s32[32,128]{1,0:T(8,128)} %bitcast.10, ...), custom_call_target="tpu_custom_call" | custom-call | tf_op jit(solution)/shard_map/advance/pallas_call | solution.py:530
  22.8 3.9 %place.1 = f32[10,3,6144]{2,1,0:T(4,128)} custom-call(s32[56,128]{1,0:T(8,128)} %get-tuple-element.9.rel, bf16[144,128]{1,0:T(8,128)(2,1)} %get-tuple-element.10.pw, f32[8,128]{1,0:T(8,128)} %get-tuple-element.11.stat, f32[1624,128]{1,0:T(8,128)} %get-tuple-element.12.st_in), custom_call_target="tpu_custom_call" | custom-call | tf_op jit(solution)/shard_map/place/pallas_call | solution.py:571

commit v3 on v2

--- a/solution.py
+++ b/solution.py
@@ -473,11 +473,8 @@
     return tiles
 
 
-def place(rel, pw, stat, st_in, out, st, new_tiles, pk, near, code, lidx, pkw, sems):
-    load = pltpu.make_async_copy(st_in, st, sems.at[0])
-    load.start()
+def place(rel, pw, stat, st, out, new_tiles, pk, near, code, lidx, pkw, sems):
     tiles = tables(stat[0:1, :], rel, pk, near, code, lidx, pkw)
-    load.wait()
     weight = pw[:, 0:96]
     stores = []
     for pair in range(24):
@@ -501,7 +498,7 @@
                 new_tiles[n, :, r * 128 : (r + 1) * 128] = new[4 * n : 4 * n + 3]
         if pair % 6 == 5:
             part = pl.ds((pair // 6) * 1536, 1536)
-            store = pltpu.make_async_copy(new_tiles.at[:, :, part], out.at[:, :, part], sems.at[1 + pair // 6])
+            store = pltpu.make_async_copy(new_tiles.at[:, :, part], out.at[:, :, part], sems.at[pair // 6])
             store.start()
             stores.append(store)
     for store in stores:
@@ -530,10 +527,10 @@
         st, pk, pw, stat = pl.pallas_call(
             functools.partial(advance, rows, cols, low),
             out_shape=[
-                jax.ShapeDtypeStruct((((placed + 1) * RP + 7) // 8 * 8, 128), f32),
-                jax.ShapeDtypeStruct((56, 128), i32),
-                jax.ShapeDtypeStruct((144, 128), bf16),
-                jax.ShapeDtypeStruct((8, 128), f32),
+                pltpu.VMEM((((placed + 1) * RP + 7) // 8 * 8, 128), f32),
+                pltpu.VMEM((56, 128), i32),
+                pltpu.VMEM((144, 128), bf16),
+                pltpu.VMEM((8, 128), f32),
             ],
             in_specs=[hbm] * 8,
             out_specs=[vm] * 4,
@@ -571,20 +568,19 @@
         new = pl.pallas_call(
             place,
             out_shape=jax.ShapeDtypeStruct((10, 3, placed * 128), f32),
-            in_specs=[vm] * 3 + [hbm],
+            in_specs=[vm] * 4,
             out_specs=hbm,
             scratch_shapes=[
-                pltpu.VMEM(st.shape, f32),
                 pltpu.VMEM((10, 3, placed * 128), f32),
                 pltpu.VMEM((56, 128), i32),
                 pltpu.VMEM((8, 128), i32),
                 pltpu.VMEM((48, 128), i32),
                 pltpu.VMEM((48, 128), i32),
                 pltpu.VMEM((2, 48, 128), i32),
-                pltpu.SemaphoreType.DMA((5,)),
+                pltpu.SemaphoreType.DMA((4,)),
             ],
             name="place",
-        )(pk, pw, stat, st)
+        )(*(pltpu.with_memory_space_constraint(a, pltpu.VMEM) for a in (pk, pw, stat, st)))
         return new.transpose(1, 0, 2)
 
     halves = ("row", "col")

time: 26.9 us -> 25 us (0.929)
  Pallas kernels: 26.7 us -> 24.9 us
    pallas_call x1, Pallas kernels: 22.8 us -> 21.8 us  [shards(): pl.pallas_call(functools.partial(advance, rows, cols, low), out_shape=[pl...]
    pallas_call x1, Pallas kernels: 3.91 us -> 3.08 us  [shards(): pl.pallas_call(place, out_shape=jax.ShapeDtypeStruct((10, 3, placed * 128...]
where the time goes in v3:
time: 25 us; the launch traced here: 24.9 us
  Pallas kernels  24.9 us (100%)
    pallas_call x1, Pallas kernels, shards(): pl.pallas_call(functools.partial(advance, rows, cols, low), out_shape=[pl...  21.8 us
    pallas_call x1, Pallas kernels, shards(): pl.pallas_call(place, out_shape=jax.ShapeDtypeStruct((10, 3, placed * 128...  3.08 us

profile of v3, /device:TPU:1, one launch (start us, length us, event | category | flops | bytes accessed | tf_op | source)
XLA Modules:
  0.0 24.9 jit_solution(16806888718995896515)
XLA Ops:
  0.0 21.8 %advance.1 = (f32[1624,128]{1,0:T(8,128)S(1)}, s32[56,128]{1,0:T(8,128)S(1)}, bf16[144,128]{1,0:T(8,128)(2,1)S(1)}, f32[8,128]{1,0:T(8,128)S(1)}) custom-call(f32[10,3,4096]{2,1,0:T(4,128)} %bitcast.7, f32[4,4096]{1,0:T(4,128)} %metric.1, f32[32,128]{1,0:T(8,128)} %bitcast.8, s32[32,128]{1,0:T(8,128)} %bitcast.9, s32[32,128]{1,0:T(8,128)} %bitcast.10, ...), custom_call_target="tpu_custom_call" | custom-call | tf_op jit(solution)/shard_map/advance/pallas_call | solution.py:527
  21.8 3.1 %place.1 = f32[10,3,6144]{2,1,0:T(4,128)} custom-call(s32[56,128]{1,0:T(8,128)S(1)} %get-tuple-element.9.rel, bf16[144,128]{1,0:T(8,128)(2,1)S(1)} %get-tuple-element.10.pw, f32[8,128]{1,0:T(8,128)S(1)} %get-tuple-element.11.stat, f32[1624,128]{1,0:T(8,128)S(1)} %get-tuple-element.12.st), custom_call_target="tpu_custom_call" | custom-call | tf_op jit(solution)/shard_map/place/pallas_call | solution.py:568

commit v4 on v3

--- a/solution.py
+++ b/solution.py
@@ -60,12 +60,12 @@
     return hi, (x - hi.astype(f32)).astype(bf16)
 
 
-def joined(own, box, size, position):
-    part = box[0 : size - 1, :]
-    member = lax.broadcasted_iota(i32, part.shape, 0) + 1
+def joined(own, box, members, earlier):
+    part = box[0:members, :]
     best = jnp.maximum(own, jnp.max(part, axis=0, keepdims=True))
     both = own + jnp.sum(part, axis=0, keepdims=True)
-    before = jnp.sum(jnp.where(member <= position, part, 0.0), axis=0, keepdims=True)
+    d = lax.broadcasted_iota(i32, part.shape, 0) + 1
+    before = jnp.sum(jnp.where(earlier(d), part, 0.0), axis=0, keepdims=True)
     return jnp.where(lanes_of((1, 128)) < 64, best, both), before
 
 
@@ -80,27 +80,38 @@
     here, send, recv, send1, recv1, send2, recv2,
 ):
     total = rows * cols
-    high = total // low
-    me = lax.axis_index("row") * cols + lax.axis_index("col")
-    lo, hi = lax.rem(me, low), me // low
-
-    def at(flat):
-        return (flat // cols, lax.rem(flat, cols))
-
-    right = at(lax.rem(me + 1, total))
-    left = at(lax.rem(me + total - 1, total))
-    peers1 = [at(hi * low + lax.rem(lo + d, low)) for d in range(1, low)]
-    peers2 = [at(lax.rem(hi + d, high) * low + lo) for d in range(1, high)]
-
-    barrier = pltpu.get_barrier_semaphore()
-    everyone = [left, right] + peers1 + peers2
-    for peer in everyone:
-        pl.semaphore_signal(barrier, inc=1, device_id=peer, device_id_type=MESH)
+    part, deep = cols // low, rows * (cols // low)
+    row, col = lax.axis_index("row"), lax.axis_index("col")
+    me = row * cols + col
+    block, lo = col // low, lax.rem(col, low)
+
+    def wrapped(x, n):
+        return jnp.where(x >= n, x - n, x)
+
+    def hops(d, n):
+        return min(d, n - d)
+
+    over = wrapped(col + 1, cols)
+    under = wrapped(col + cols - 1, cols)
+    right = (jnp.where(over == 0, wrapped(row + 1, rows), row), over)
+    left = (jnp.where(col == 0, wrapped(row + rows - 1, rows), row), under)
+    near = sorted(range(1, low), key=lambda d: -hops(d // 2, low // 2))
+    peers1 = {d: (row, block * low + wrapped(lo + d, low)) for d in near}
+    row_at = [wrapped(row + d, rows) for d in range(rows)]
+    col_at = [wrapped(block + d, part) * low + lo for d in range(part)]
+    far = sorted(range(1, deep), key=lambda d: -hops(d // part, rows) - hops(d % part, part))
+    peers2 = {d: (row_at[d // part], col_at[d % part]) for d in far}
+    everyone = [peers1[d] for d in near] + [peers2[d] for d in far] + [left, right]
 
     pairs = (
         (metric, gv), (depth, dv), (refine, bv), (state, sv), (partner, av), (diff_ops, wd), (lift, wt), (prolong, wc))
     loads = [pltpu.make_async_copy(a, b, here.at[k]) for k, (a, b) in enumerate(pairs)]
-    for load in loads:
+    for load in loads[:3]:
+        load.start()
+    barrier = pltpu.get_barrier_semaphore()
+    for peer in everyone:
+        pl.semaphore_signal(barrier, inc=1, device_id=peer, device_id_type=MESH)
+    for load in loads[3:]:
         load.start()
     for load in loads[:3]:
         load.wait()
@@ -118,9 +129,9 @@
     def round_of(source, box, peers, sems, rems):
         return [
             pltpu.make_async_remote_copy(
-                src_ref=source.at[pl.ds(0, 1)], dst_ref=box.at[pl.ds(d, 1)], send_sem=sems.at[d], recv_sem=rems.at[d],
-                device_id=peer, device_id_type=MESH)
-            for d, peer in enumerate(peers)
+                src_ref=source.at[pl.ds(0, 1)], dst_ref=box.at[pl.ds(d - 1, 1)],
+                send_sem=sems.at[d - 1], recv_sem=rems.at[d - 1], device_id=peer, device_id_type=MESH)
+            for d, peer in peers.items()
         ]
 
     round1 = round_of(mine, box1, peers1, send1, recv1)
@@ -160,18 +171,24 @@
     for g in (3, 4):
         first_rate(g)
     child_weights(wc, pw, tmp, wf)
+
+    def earlier2(d):
+        r, b = row - d // part, block - d % part
+        r, b = jnp.where(r < 0, r + rows, r), jnp.where(b < 0, b + part, b)
+        return r * part + b < row * part + block
+
+    for copy in round1:
+        copy.wait_recv()
+    own, before1 = joined(own, box1, low - 1, lambda d: d <= lo)
+    mine2[0:1, :] = own
+    for copy in round2:
+        copy.start()
     for copy in copies:
         copy.wait_recv()
     load_rims((ls, lm, ld, lp), (rs, rm, rd, rp), qt, mt, cv, pv, ends)
     mirror(qt, QP, state_row, mt, ends)
     for g in (2, 5, 6, 1, 0):
         first_rate(g)
-    for copy in round1:
-        copy.wait_recv()
-    own, before1 = joined(own, box1, low, lo)
-    mine2[0:1, :] = own
-    for copy in round2:
-        copy.start()
     r1[64 * RP : 65 * RP, :] = r1[8 * RP : 9 * RP, :]
     mirror(r1, RP, result_row, mt, ends)
     for g in range(1, 7):
@@ -179,9 +196,11 @@
         flux(m, r1, RP, result_row, mt, cv, pv, co, xt, 8 * (g % 2))
         product(m, 8 * (g % 2), xt, wl, r2)
     prefix(lr, bv, rr, rv, pk)
+    for copy in round1 + round2 + copies:
+        copy.wait_send()
     for copy in round2:
         copy.wait_recv()
-    own, before2 = joined(own, box2, high, hi)
+    own, before2 = joined(own, box2, deep - 1, earlier2)
     best = jnp.where(half, own, pltpu.roll(own, 64, 1))
     before = before1 + before2
     before = jnp.where(half, pltpu.roll(before, 64, 1), before)
@@ -189,8 +208,6 @@
     step = COURANT / best
     for g in range(1, 7):
         combine(8 + 8 * g, step, qt, r1, r2, st)
-    for copy in round1 + round2 + copies:
-        copy.wait_send()
 
 
 def wave_rate(depth, grads):
@@ -508,7 +525,7 @@
 def solution(mesh):
     rows, cols = mesh.shape["row"], mesh.shape["col"]
     total = rows * cols
-    low = 16 if total % 256 == 0 else max(total // 2, 1)
+    low = min(16, cols // 2)
     high = total // low
     placed = OWN + OWN // 2
 

time: 25 us -> 22.3 us (0.89)
  Pallas kernels: 24.9 us -> 22.2 us
    pallas_call x1, Pallas kernels: 21.8 us -> 19.2 us  [shards(): pl.pallas_call(functools.partial(advance, rows, cols, low), out_shape=[pl...]
where the time goes in v4:
time: 22.3 us; the launch traced here: 22.2 us
  Pallas kernels  22.2 us (100%)
    pallas_call x1, Pallas kernels, shards(): pl.pallas_call(functools.partial(advance, rows, cols, low), out_shape=[pl...  19.2 us
    pallas_call x1, Pallas kernels, shards(): pl.pallas_call(place, out_shape=jax.ShapeDtypeStruct((10, 3, placed * 128...  3.08 us

profile of v4, /device:TPU:1, one launch (start us, length us, event | category | flops | bytes accessed | tf_op | source)
XLA Modules:
  0.0 22.2 jit_solution(4087695011453632292)
XLA Ops:
  0.0 19.2 %advance.1 = (f32[1624,128]{1,0:T(8,128)S(1)}, s32[56,128]{1,0:T(8,128)S(1)}, bf16[144,128]{1,0:T(8,128)(2,1)S(1)}, f32[8,128]{1,0:T(8,128)S(1)}) custom-call(f32[10,3,4096]{2,1,0:T(4,128)} %bitcast.7, f32[4,4096]{1,0:T(4,128)} %metric.1, f32[32,128]{1,0:T(8,128)} %bitcast.8, s32[32,128]{1,0:T(8,128)} %bitcast.9, s32[32,128]{1,0:T(8,128)} %bitcast.10, ...), custom_call_target="tpu_custom_call" | custom-call | tf_op jit(solution)/shard_map/advance/pallas_call | solution.py:544
  19.2 3.1 %place.1 = f32[10,3,6144]{2,1,0:T(4,128)} custom-call(s32[56,128]{1,0:T(8,128)S(1)} %get-tuple-element.9.rel, bf16[144,128]{1,0:T(8,128)(2,1)S(1)} %get-tuple-element.10.pw, f32[8,128]{1,0:T(8,128)S(1)} %get-tuple-element.11.stat, f32[1624,128]{1,0:T(8,128)S(1)} %get-tuple-element.12.st), custom_call_target="tpu_custom_call" | custom-call | tf_op jit(solution)/shard_map/place/pallas_call | solution.py:585

commit v5 on v4

--- a/solution.py
+++ b/solution.py
@@ -72,10 +72,10 @@
 def advance(
     rows, cols, low,
     state, metric, depth, partner, refine, diff_ops, lift, prolong,
-    st, pk, pw, stat,
+    st, tab, pw, stat,
     sv, gv, dv, av, bv, wd, wt, wc,
     ls, lm, ld, lp, lr, rs, rm, rd, rp, rr,
-    qt, mt, cv, pv, co, xt, r1, r2, wl, tmp, wf, rv,
+    qt, mt, cv, pv, co, xt, r1, r2, wl, tmp, wf, rv, pk, pkw,
     mine, box1, mine2, box2,
     here, send, recv, send1, recv1, send2, recv2,
 ):
@@ -95,13 +95,13 @@
     under = wrapped(col + cols - 1, cols)
     right = (jnp.where(over == 0, wrapped(row + 1, rows), row), over)
     left = (jnp.where(col == 0, wrapped(row + rows - 1, rows), row), under)
-    near = sorted(range(1, low), key=lambda d: -hops(d // 2, low // 2))
-    peers1 = {d: (row, block * low + wrapped(lo + d, low)) for d in near}
+    close = sorted(range(1, low), key=lambda d: -hops(d // 2, low // 2))
+    peers1 = {d: (row, block * low + wrapped(lo + d, low)) for d in close}
     row_at = [wrapped(row + d, rows) for d in range(rows)]
     col_at = [wrapped(block + d, part) * low + lo for d in range(part)]
     far = sorted(range(1, deep), key=lambda d: -hops(d // part, rows) - hops(d % part, part))
     peers2 = {d: (row_at[d // part], col_at[d % part]) for d in far}
-    everyone = [peers1[d] for d in near] + [peers2[d] for d in far] + [left, right]
+    everyone = [peers1[d] for d in close] + [peers2[d] for d in far] + [left, right]
 
     pairs = (
         (metric, gv), (depth, dv), (refine, bv), (state, sv), (partner, av), (diff_ops, wd), (lift, wt), (prolong, wc))
@@ -196,6 +196,7 @@
         flux(m, r1, RP, result_row, mt, cv, pv, co, xt, 8 * (g % 2))
         product(m, 8 * (g % 2), xt, wl, r2)
     prefix(lr, bv, rr, rv, pk)
+    tables(pk, pkw, tab)
     for copy in round1 + round2 + copies:
         copy.wait_send()
     for copy in round2:
@@ -456,42 +457,62 @@
     lower = lanes_of((48, 48)) < lax.broadcasted_iota(i32, (48, 48), 0)
     before = jnp.dot(lower.astype(f32).astype(bf16), sums.astype(bf16), preferred_element_type=f32)
     ends = (within + before - before[8:9, :]).astype(i32)
-    pk[0:48, :] = 2 * (ends - 1 - bits) + bits
-    pk[48:56, :] = jnp.full((8, 128), 1 << 21, i32)
-
-
-def tables(offset, rel, pk, near, code, lidx, pkw):
-    pk[...] = rel[...] + 2 * offset.astype(i32)
-    ends = (pk[0:48, :] >> 1) + 1 + (pk[0:48, :] & 1)
+    pk[...] = 2 * (ends - 1 - bits) + bits
+
+
+def tables(pk, pkw, tab):
+    row = lax.broadcasted_iota(i32, (48, 128), 0)
+    ends = (pk[...] >> 1) + 1 + (pk[...] & 1)
     last = jnp.broadcast_to(ends[:, 127:128], (48, 128))
-    reached = (last <= lanes_of((48, 128)) * 128).astype(f32)
-    first = jnp.sum(reached, axis=0, keepdims=True).astype(i32)
-    near[...] = jnp.broadcast_to(first, (8, 128))
-    tiles = [near[0, r] for r in range(48)]
-    for r in range(48):
-        pkw[0, r : r + 1, :] = pk[pl.ds(tiles[r], 1), :]
-        pkw[1, r : r + 1, :] = pk[pl.ds(tiles[r] + 1, 1), :]
-    for g in range(6):
+    reached = jnp.where(last <= lanes_of((48, 128)) * 128 - 1024, 1.0, 0.0)
+    here = jnp.where(row == 0, 1.0, pltpu.roll(reached, 1, 0)) - reached
+    after = jnp.where(row == 0, 0.0, pltpu.roll(here, 1, 0))
+    shifted = pk[...] + 8192
+    tiles = [(shifted >> 8), shifted & 255, row]
+    tiles = jnp.concatenate([t.astype(f32).astype(bf16) for t in tiles], axis=1)
+    for i, mark in enumerate((here, after)):
+        found = jnp.dot(mark.T[0:64].astype(bf16), tiles, preferred_element_type=f32).astype(i32)
+        pkw[i, :, :] = found[:, 0:128] * 256 + found[:, 128:256] - 8192
+        if i == 0:
+            pkw[2, :, :] = found[:, 256:384] * 128
+    for g in range(8):
         rows = slice(8 * g, 8 * g + 8)
         p0, p1 = pkw[0, rows, :], pkw[1, rows, :]
         e0 = (p0 >> 1) + 1 + (p0 & 1)
         e1 = (p1 >> 1) + 1 + (p1 & 1)
-        slot = (8 * g + lax.broadcasted_iota(i32, (8, 128), 0)) * 128 + lanes_of((8, 128))
+        slot = (8 * g - 8 + lax.broadcasted_iota(i32, (8, 128), 0)) * 128 + lanes_of((8, 128))
         over = jnp.broadcast_to(e0[:, 127:128], (8, 128)) <= slot
         pos = jnp.zeros((8, 128), i32)
         for s in (64, 32, 16, 8, 4, 2, 1):
             probe = pos + (s - 1)
             e = jnp.where(over, pick(e1, probe), pick(e0, probe))
             pos = jnp.where(e <= slot, pos + s, pos)
+        pos = jnp.minimum(pos, 127)
         got = jnp.where(over, pick(p1, pos), pick(p0, pos))
         which = slot - (got >> 1)
-        lidx[rows, :] = jnp.where(over, pos + 128, pos)
-        code[rows, :] = jnp.where((got & 1) == 0, 0, 1 + which)
-    return tiles
-
-
-def place(rel, pw, stat, st, out, new_tiles, pk, near, code, lidx, pkw, sems):
-    tiles = tables(stat[0:1, :], rel, pk, near, code, lidx, pkw)
+        parent = pkw[2, rows, :] + jnp.where(over, pos + 128, pos)
+        tab[rows, :] = 4 * parent + jnp.where((got & 1) == 0, 0, 1 + which)
+
+
+def aligned(offset, tab, near, code, lidx):
+    near[0:8, :] = jnp.broadcast_to(1024 - offset.astype(i32), (8, 128))
+    begin = near[0, 0]
+    row, turn = jnp.clip(begin >> 7, 0, 16), begin & 127
+    back = (128 - turn) & 127
+    keep = lanes_of((8, 128)) >= turn
+    for g in range(6):
+        rows = slice(8 * g, 8 * g + 8)
+        both = jnp.where(keep, tab[pl.ds(row + 8 * g, 8), :], tab[pl.ds(row + 8 * g + 1, 8), :])
+        both = pltpu.roll(both, back, 1)
+        tile = jnp.clip(jnp.broadcast_to(both[:, 0:1], (8, 128)) >> 9, 0, 47)
+        lidx[rows, :] = (both >> 2) - tile * 128
+        code[rows, :] = both & 3
+        near[rows, :] = tile
+    return [near[r, 0] for r in range(48)]
+
+
+def place(tab, pw, stat, st, out, new_tiles, near, code, lidx, sems):
+    tiles = aligned(stat[0:1, :], tab, near, code, lidx)
     weight = pw[:, 0:96]
     stores = []
     for pair in range(24):
@@ -513,9 +534,11 @@
             new = jnp.where(kind == 0, one[0:48], jnp.where(kind == 1, one[48:96], one[96:144]))
             for n in range(10):
                 new_tiles[n, :, r * 128 : (r + 1) * 128] = new[4 * n : 4 * n + 3]
-        if pair % 6 == 5:
-            part = pl.ds((pair // 6) * 1536, 1536)
-            store = pltpu.make_async_copy(new_tiles.at[:, :, part], out.at[:, :, part], sems.at[pair // 6])
+        if pair in (7, 15, 20, 23):
+            k = len(stores)
+            begin = (0, 8, 16, 21)[k]
+            part = pl.ds(begin * 256, (pair + 1 - begin) * 256)
+            store = pltpu.make_async_copy(new_tiles.at[:, :, part], out.at[:, :, part], sems.at[k])
             store.start()
             stores.append(store)
     for store in stores:
@@ -541,11 +564,11 @@
             pltpu.VMEM((16, 128), i32),
             pltpu.VMEM((16, 128), i32),
         ]
-        st, pk, pw, stat = pl.pallas_call(
+        st, tab, pw, stat = pl.pallas_call(
             functools.partial(advance, rows, cols, low),
             out_shape=[
                 pltpu.VMEM((((placed + 1) * RP + 7) // 8 * 8, 128), f32),
-                pltpu.VMEM((56, 128), i32),
+                pltpu.VMEM((72, 128), i32),
                 pltpu.VMEM((144, 128), bf16),
                 pltpu.VMEM((8, 128), f32),
             ],
@@ -567,6 +590,8 @@
                 pltpu.VMEM((16, 128), f32),
                 pltpu.VMEM((48, 128), f32),
                 pltpu.VMEM((48, 128), i32),
+                pltpu.VMEM((48, 128), i32),
+                pltpu.VMEM((3, 64, 128), i32),
                 pltpu.VMEM((8, 128), f32),
                 pltpu.VMEM((low, 128), f32),
                 pltpu.VMEM((8, 128), f32),
@@ -589,15 +614,13 @@
             out_specs=hbm,
             scratch_shapes=[
                 pltpu.VMEM((10, 3, placed * 128), f32),
-                pltpu.VMEM((56, 128), i32),
-                pltpu.VMEM((8, 128), i32),
                 pltpu.VMEM((48, 128), i32),
                 pltpu.VMEM((48, 128), i32),
-                pltpu.VMEM((2, 48, 128), i32),
+                pltpu.VMEM((48, 128), i32),
                 pltpu.SemaphoreType.DMA((4,)),
             ],
             name="place",
-        )(*(pltpu.with_memory_space_constraint(a, pltpu.VMEM) for a in (pk, pw, stat, st)))
+        )(*(pltpu.with_memory_space_constraint(a, pltpu.VMEM) for a in (tab, pw, stat, st)))
         return new.transpose(1, 0, 2)
 
     halves = ("row", "col")

time: 22.3 us -> 22.1 us (level)
    pallas_call x1, Pallas kernels: 3.08 us -> 1.88 us  [shards(): pl.pallas_call(place, out_shape=jax.ShapeDtypeStruct((10, 3, placed * 128...]
    pallas_call x1, Pallas kernels: 19.2 us -> 20.1 us  [shards(): pl.pallas_call(functools.partial(advance, rows, cols, low), out_shape=[pl...]
where the time goes in v5:
time: 22.1 us; the launch traced here: 22 us
  Pallas kernels  22 us (100%)
    pallas_call x1, Pallas kernels, shards(): pl.pallas_call(functools.partial(advance, rows, cols, low), out_shape=[pl...  20.1 us
    pallas_call x1, Pallas kernels, shards(): pl.pallas_call(place, out_shape=jax.ShapeDtypeStruct((10, 3, placed * 128...  1.88 us

profile of v5, /device:TPU:1, one launch (start us, length us, event | category | flops | bytes accessed | tf_op | source)
XLA Modules:
  0.0 22.0 jit_solution(9082164904099144372)
XLA Ops:
  0.0 20.1 %advance.1 = (f32[1624,128]{1,0:T(8,128)S(1)}, s32[72,128]{1,0:T(8,128)S(1)}, bf16[144,128]{1,0:T(8,128)(2,1)S(1)}, f32[8,128]{1,0:T(8,128)S(1)}) custom-call(f32[10,3,4096]{2,1,0:T(4,128)} %bitcast.7, f32[4,4096]{1,0:T(4,128)} %metric.1, f32[32,128]{1,0:T(8,128)} %bitcast.8, s32[32,128]{1,0:T(8,128)} %bitcast.9, s32[32,128]{1,0:T(8,128)} %bitcast.10, ...), custom_call_target="tpu_custom_call" | custom-call | tf_op jit(solution)/shard_map/advance/pallas_call | solution.py:567
  20.1 1.9 %place.1 = f32[10,3,6144]{2,1,0:T(4,128)} custom-call(s32[72,128]{1,0:T(8,128)S(1)} %get-tuple-element.9.tab, bf16[144,128]{1,0:T(8,128)(2,1)S(1)} %get-tuple-element.10.pw, f32[8,128]{1,0:T(8,128)S(1)} %get-tuple-element.11.stat, f32[1624,128]{1,0:T(8,128)S(1)} %get-tuple-element.12.st), custom_call_target="tpu_custom_call" | custom-call | tf_op jit(solution)/shard_map/place/pallas_call | solution.py:610

commit v6 on v5

--- a/solution.py
+++ b/solution.py
@@ -14,8 +14,9 @@
 OWN = 32
 HALO = 9
 WIDE = HALO * 128
-BASE = 24
-MEM = 72
+BASE = 2
+RING = BASE + OWN + 2 * HALO
+MEM = 64
 QP = 41
 RR = 32
 RP = 33
@@ -161,15 +162,25 @@
         lay_state(qt, BASE + t, sv, t)
     cv[BASE : BASE + OWN, :] = GRAVITY * dv[...]
     pv[BASE : BASE + OWN, :] = av[...]
-
-    def first_rate(g):
-        m = 8 + 8 * g
-        coefficients(m, mt, cv, pv, co)
-        flux(m, qt, QP, state_row, mt, cv, pv, co, xt, 8 * (g % 2))
-        product(m, 8 * (g % 2), xt, wl, r1)
-
-    for g in (3, 4):
-        first_rate(g)
+    for t in range(4):
+        lay_state(qt, RING + t, sv, t)
+        lay_metric(mt, RING + t, gv, t)
+    cv[RING : RING + 4, :] = GRAVITY * dv[0:4, :]
+    pv[RING : RING + 4, :] = av[0:4, :]
+
+    def first_rates(tiles):
+        for i, m in enumerate(tiles):
+            coefficients(m, mt, cv, pv, co)
+            flux(m, qt, QP, state_row, mt, cv, pv, co, xt, 8 * (i % 2))
+            product(m, 8 * (i % 2), xt, wl, r1)
+
+    def second_rates(tiles):
+        for i, m in enumerate(tiles):
+            flux(m, r1, RP, result_row, mt, cv, pv, co, xt, 8 * (i % 2))
+            product(m, 8 * (i % 2), xt, wl, r2)
+
+    first_rates((BASE + 1, BASE + 9, BASE + 17, BASE + 23))
+    second_rates((BASE + 2, BASE + 10, BASE + 18, BASE + 22))
     child_weights(wc, pw, tmp, wf)
 
     def earlier2(d):
@@ -187,14 +198,12 @@
         copy.wait_recv()
     load_rims((ls, lm, ld, lp), (rs, rm, rd, rp), qt, mt, cv, pv, ends)
     mirror(qt, QP, state_row, mt, ends)
-    for g in (2, 5, 6, 1, 0):
-        first_rate(g)
-    r1[64 * RP : 65 * RP, :] = r1[8 * RP : 9 * RP, :]
+    first_rates((BASE + 30, BASE + 38, BASE + 46))
     mirror(r1, RP, result_row, mt, ends)
-    for g in range(1, 7):
-        m = 8 + 8 * g
-        flux(m, r1, RP, result_row, mt, cv, pv, co, xt, 8 * (g % 2))
-        product(m, 8 * (g % 2), xt, wl, r2)
+    second_rates((BASE + 30, BASE + 38, BASE + 44))
+    r1[BASE * RP : BASE * RP + RR, :] = r1[RING * RP : RING * RP + RR, :]
+    for t in range(2):
+        r2[(BASE + t) * RP : (BASE + t) * RP + RR, :] = r2[(RING + t) * RP : (RING + t) * RP + RR, :]
     prefix(lr, bv, rr, rv, pk)
     tables(pk, pkw, tab)
     for copy in round1 + round2 + copies:
@@ -207,8 +216,9 @@
     before = jnp.where(half, pltpu.roll(before, 64, 1), before)
     stat[0:1, :] = before - (me * (OWN * 64)).astype(f32)
     step = COURANT / best
-    for g in range(1, 7):
-        combine(8 + 8 * g, step, qt, r1, r2, st)
+    combine(RING - 8, 0, step, qt, r1, r2, st)
+    for g in range(5):
+        combine(BASE + 8 * g, 8 + 8 * g, step, qt, r1, r2, st)
 
 
 def wave_rate(depth, grads):
@@ -235,23 +245,16 @@
         lay_metric(mt, m, g, t)
 
     for t in range(HALO):
-        lay(BASE - HALO + t, ls, lm, t)
-        if t < HALO - 1:
-            lay(BASE + OWN + t, rs, rm, t)
-    lay(8, rs, rm, HALO - 1)
-    lay(64, rs, rm, HALO - 1)
-    lay(7, rs, rm, HALO - 2)
+        lay(RING - HALO + t, ls, lm, t)
+        lay(BASE + OWN + t, rs, rm, t)
     for into, before, after, scale in ((cv, ld, rd, GRAVITY), (pv, lp, rp, 1)):
-        into[BASE - HALO : BASE, :] = scale * before[16 - HALO : 16, :]
-        into[BASE + OWN : BASE + OWN + 8, :] = scale * after[0:8, :]
-        into[7:8, :] = scale * after[7:8, :]
-        into[8:9, :] = scale * after[8:9, :]
-        into[64:65, :] = scale * after[8:9, :]
+        into[RING - HALO : RING, :] = scale * before[16 - HALO : 16, :]
+        into[BASE + OWN : BASE + OWN + HALO, :] = scale * after[0:HALO, :]
     first, last = ends
 
     @pl.when(first)
     def _():
-        cv[BASE - 1 : BASE, :] = pltpu.roll(cv[BASE : BASE + 1, :], 127, 1)
+        cv[RING - 1 : RING, :] = pltpu.roll(cv[RING : RING + 1, :], 127, 1)
 
     @pl.when(last)
     def _():
@@ -283,8 +286,8 @@
 
     @pl.when(first)
     def _():
-        _, _, sx, sy = grads(BASE)
-        write(BASE, BASE - 1, FACES[0], MEET[0], -sx, -sy, 127, 127)
+        _, _, sx, sy = grads(RING)
+        write(RING, RING - 1, FACES[0], MEET[0], -sx, -sy, 127, 127)
 
     @pl.when(last)
     def _():
@@ -434,15 +437,15 @@
         pw[i * 48 : i * 48 + 48, :] = (hi + pltpu.roll(hi, 32, 1) + pltpu.roll(low, 64, 1)).astype(bf16)
 
 
-def combine(m, step, qt, r1, r2, st):
+def combine(m, to, step, qt, r1, r2, st):
     half = 0.5 * step * step
     for f in range(3):
         for n in range(10):
             v = f * 10 + n
             x = spread(qt, state_row(f, n), m, QP) + (step * spread(r1, v, m, RP) + half * spread(r2, v, m, RP))
-            put(st, v, m - 16, RP, x)
-    put(st, 30, m - 16, RP, jnp.zeros((8, 128), f32))
-    put(st, 31, m - 16, RP, jnp.zeros((8, 128), f32))
+            put(st, v, to, RP, x)
+    put(st, 30, to, RP, jnp.zeros((8, 128), f32))
+    put(st, 31, to, RP, jnp.zeros((8, 128), f32))
 
 
 def prefix(lr, refine, rr, rv, pk):

time: 22.1 us -> 21.3 us (0.964)
  Pallas kernels: 22 us -> 21.2 us
    pallas_call x1, Pallas kernels: 20.1 us -> 19.3 us  [shards(): pl.pallas_call(functools.partial(advance, rows, cols, low), out_shape=[pl...]
where the time goes in v6:
time: 21.3 us; the launch traced here: 21.2 us
  Pallas kernels  21.2 us (100%)
    pallas_call x1, Pallas kernels, shards(): pl.pallas_call(functools.partial(advance, rows, cols, low), out_shape=[pl...  19.3 us
    pallas_call x1, Pallas kernels, shards(): pl.pallas_call(place, out_shape=jax.ShapeDtypeStruct((10, 3, placed * 128...  1.88 us

profile of v6, /device:TPU:1, one launch (start us, length us, event | category | flops | bytes accessed | tf_op | source)
XLA Modules:
  0.0 21.2 jit_solution(5494303131911493667)
XLA Ops:
  0.0 19.3 %advance.1 = (f32[1624,128]{1,0:T(8,128)S(1)}, s32[72,128]{1,0:T(8,128)S(1)}, bf16[144,128]{1,0:T(8,128)(2,1)S(1)}, f32[8,128]{1,0:T(8,128)S(1)}) custom-call(f32[10,3,4096]{2,1,0:T(4,128)} %bitcast.7, f32[4,4096]{1,0:T(4,128)} %metric.1, f32[32,128]{1,0:T(8,128)} %bitcast.8, s32[32,128]{1,0:T(8,128)} %bitcast.9, s32[32,128]{1,0:T(8,128)} %bitcast.10, ...), custom_call_target="tpu_custom_call" | custom-call | tf_op jit(solution)/shard_map/advance/pallas_call | solution.py:570
  19.4 1.9 %place.1 = f32[10,3,6144]{2,1,0:T(4,128)} custom-call(s32[72,128]{1,0:T(8,128)S(1)} %get-tuple-element.9.tab, bf16[144,128]{1,0:T(8,128)(2,1)S(1)} %get-tuple-element.10.pw, f32[8,128]{1,0:T(8,128)S(1)} %get-tuple-element.11.stat, f32[1624,128]{1,0:T(8,128)S(1)} %get-tuple-element.12.st), custom_call_target="tpu_custom_call" | custom-call | tf_op jit(solution)/shard_map/place/pallas_call | solution.py:613

commit v7 on v6

--- a/solution.py
+++ b/solution.py
@@ -96,13 +96,14 @@
     under = wrapped(col + cols - 1, cols)
     right = (jnp.where(over == 0, wrapped(row + 1, rows), row), over)
     left = (jnp.where(col == 0, wrapped(row + rows - 1, rows), row), under)
+    has_left, has_right = me != 0, me != total - 1
     close = sorted(range(1, low), key=lambda d: -hops(d // 2, low // 2))
     peers1 = {d: (row, block * low + wrapped(lo + d, low)) for d in close}
     row_at = [wrapped(row + d, rows) for d in range(rows)]
     col_at = [wrapped(block + d, part) * low + lo for d in range(part)]
     far = sorted(range(1, deep), key=lambda d: -hops(d // part, rows) - hops(d % part, part))
     peers2 = {d: (row_at[d // part], col_at[d % part]) for d in far}
-    everyone = [peers1[d] for d in close] + [peers2[d] for d in far] + [left, right]
+    everyone = [peers1[d] for d in close] + [peers2[d] for d in far]
 
     pairs = (
         (metric, gv), (depth, dv), (refine, bv), (state, sv), (partner, av), (diff_ops, wd), (lift, wt), (prolong, wc))
@@ -112,6 +113,15 @@
     barrier = pltpu.get_barrier_semaphore()
     for peer in everyone:
         pl.semaphore_signal(barrier, inc=1, device_id=peer, device_id_type=MESH)
+
+    @pl.when(has_left)
+    def _():
+        pl.semaphore_signal(barrier, inc=1, device_id=left, device_id_type=MESH)
+
+    @pl.when(has_right)
+    def _():
+        pl.semaphore_signal(barrier, inc=1, device_id=right, device_id_type=MESH)
+
     for load in loads[3:]:
         load.start()
     for load in loads[:3]:
@@ -150,9 +160,17 @@
                 src_ref=source, dst_ref=target, send_sem=send.at[k], recv_sem=recv.at[k],
                 device_id=peer, device_id_type=MESH))
 
-    pl.semaphore_wait(barrier, len(everyone))
-    for copy in round1 + copies:
+    onward, back = copies[:5], copies[5:]
+
+    def each(batch, act):
+        for copy in batch:
+            act(copy)
+
+    pl.semaphore_wait(barrier, len(everyone) + has_left.astype(i32) + has_right.astype(i32))
+    for copy in round1:
         copy.start()
+    pl.when(has_right)(lambda: each(onward, lambda copy: copy.start()))
+    pl.when(has_left)(lambda: each(back, lambda copy: copy.start()))
 
     for load in loads[3:]:
         load.wait()
@@ -194,8 +212,17 @@
     mine2[0:1, :] = own
     for copy in round2:
         copy.start()
-    for copy in copies:
-        copy.wait_recv()
+    pl.when(has_left)(lambda: each(onward, lambda copy: copy.wait_recv()))
+    pl.when(has_right)(lambda: each(back, lambda copy: copy.wait_recv()))
+
+    @pl.when(~has_left)
+    def _():
+        lr[...] = jnp.zeros_like(lr)
+
+    @pl.when(~has_right)
+    def _():
+        rr[...] = jnp.zeros_like(rr)
+
     load_rims((ls, lm, ld, lp), (rs, rm, rd, rp), qt, mt, cv, pv, ends)
     mirror(qt, QP, state_row, mt, ends)
     first_rates((BASE + 30, BASE + 38, BASE + 46))
@@ -206,8 +233,10 @@
         r2[(BASE + t) * RP : (BASE + t) * RP + RR, :] = r2[(RING + t) * RP : (RING + t) * RP + RR, :]
     prefix(lr, bv, rr, rv, pk)
     tables(pk, pkw, tab)
-    for copy in round1 + round2 + copies:
+    for copy in round1 + round2:
         copy.wait_send()
+    pl.when(has_right)(lambda: each(onward, lambda copy: copy.wait_send()))
+    pl.when(has_left)(lambda: each(back, lambda copy: copy.wait_send()))
     for copy in round2:
         copy.wait_recv()
     own, before2 = joined(own, box2, deep - 1, earlier2)

time: 21.3 us -> 21.2 us (level)
  no operation moved by 1% of the time
where the time goes in v7:
time: 21.2 us; the launch traced here: 21.1 us
  Pallas kernels  21.1 us (100%)
    pallas_call x1, Pallas kernels, shards(): pl.pallas_call(functools.partial(advance, rows, cols, low), out_shape=[pl...  19.2 us
    pallas_call x1, Pallas kernels, shards(): pl.pallas_call(place, out_shape=jax.ShapeDtypeStruct((10, 3, placed * 128...  1.9 us

profile of v7, /device:TPU:1, one launch (start us, length us, event | category | flops | bytes accessed | tf_op | source)
XLA Modules:
  0.0 21.1 jit_solution(4965386024255620551)
XLA Ops:
  0.0 19.2 %advance.1 = (f32[1624,128]{1,0:T(8,128)S(1)}, s32[72,128]{1,0:T(8,128)S(1)}, bf16[144,128]{1,0:T(8,128)(2,1)S(1)}, f32[8,128]{1,0:T(8,128)S(1)}) custom-call(f32[10,3,4096]{2,1,0:T(4,128)} %bitcast.7, f32[4,4096]{1,0:T(4,128)} %metric.1, f32[32,128]{1,0:T(8,128)} %bitcast.8, s32[32,128]{1,0:T(8,128)} %bitcast.9, s32[32,128]{1,0:T(8,128)} %bitcast.10, ...), custom_call_target="tpu_custom_call" | custom-call | tf_op jit(solution)/shard_map/advance/pallas_call | solution.py:599
  19.2 1.9 %place.1 = f32[10,3,6144]{2,1,0:T(4,128)} custom-call(s32[72,128]{1,0:T(8,128)S(1)} %get-tuple-element.9.tab, bf16[144,128]{1,0:T(8,128)(2,1)S(1)} %get-tuple-element.10.pw, f32[8,128]{1,0:T(8,128)S(1)} %get-tuple-element.11.stat, f32[1624,128]{1,0:T(8,128)S(1)} %get-tuple-element.12.st), custom_call_target="tpu_custom_call" | custom-call | tf_op jit(solution)/shard_map/place/pallas_call | solution.py:642

commit v8 on v7

--- a/solution.py
+++ b/solution.py
@@ -141,10 +141,18 @@
         return [
             pltpu.make_async_remote_copy(
                 src_ref=source.at[pl.ds(0, 1)], dst_ref=box.at[pl.ds(d - 1, 1)],
-                send_sem=sems.at[d - 1], recv_sem=rems.at[d - 1], device_id=peer, device_id_type=MESH)
+                send_sem=sems.at[0], recv_sem=rems.at[0], device_id=peer, device_id_type=MESH)
             for d, peer in peers.items()
         ]
 
+    def whole(box, peers, sems, rems):
+        rows_in = box.at[pl.ds(0, len(peers))]
+        return pltpu.make_async_remote_copy(
+            src_ref=rows_in, dst_ref=rows_in, send_sem=sems.at[0], recv_sem=rems.at[0],
+            device_id=peers[1], device_id_type=MESH)
+
+    level1 = whole(box1, peers1, send1, recv1)
+    level2 = whole(box2, peers2, send2, recv2)
     round1 = round_of(mine, box1, peers1, send1, recv1)
     round2 = round_of(mine2, box2, peers2, send2, recv2)
     tail, head = pl.ds((OWN - HALO) * 128, WIDE), pl.ds(0, WIDE)
@@ -206,8 +214,7 @@
         r, b = jnp.where(r < 0, r + rows, r), jnp.where(b < 0, b + part, b)
         return r * part + b < row * part + block
 
-    for copy in round1:
-        copy.wait_recv()
+    level1.wait_recv()
     own, before1 = joined(own, box1, low - 1, lambda d: d <= lo)
     mine2[0:1, :] = own
     for copy in round2:
@@ -233,12 +240,11 @@
         r2[(BASE + t) * RP : (BASE + t) * RP + RR, :] = r2[(RING + t) * RP : (RING + t) * RP + RR, :]
     prefix(lr, bv, rr, rv, pk)
     tables(pk, pkw, tab)
-    for copy in round1 + round2:
-        copy.wait_send()
+    level1.wait_send()
+    level2.wait_send()
     pl.when(has_right)(lambda: each(onward, lambda copy: copy.wait_send()))
     pl.when(has_left)(lambda: each(back, lambda copy: copy.wait_send()))
-    for copy in round2:
-        copy.wait_recv()
+    level2.wait_recv()
     own, before2 = joined(own, box2, deep - 1, earlier2)
     best = jnp.where(half, own, pltpu.roll(own, 64, 1))
     before = before1 + before2
@@ -631,10 +637,10 @@
                 pltpu.SemaphoreType.DMA((8,)),
                 pltpu.SemaphoreType.DMA((10,)),
                 pltpu.SemaphoreType.DMA((10,)),
-                pltpu.SemaphoreType.DMA((low - 1,)),
-                pltpu.SemaphoreType.DMA((low - 1,)),
-                pltpu.SemaphoreType.DMA((high - 1,)),
-                pltpu.SemaphoreType.DMA((high - 1,)),
+                pltpu.SemaphoreType.DMA((1,)),
+                pltpu.SemaphoreType.DMA((1,)),
+                pltpu.SemaphoreType.DMA((1,)),
+                pltpu.SemaphoreType.DMA((1,)),
             ],
             compiler_params=pltpu.CompilerParams(collective_id=0, has_side_effects=True),
             name="advance",

time: 21.2 us -> 20.6 us (0.972)
  Pallas kernels: 21.1 us -> 20.5 us
    pallas_call x1, Pallas kernels: 19.2 us -> 18.6 us  [shards(): pl.pallas_call(functools.partial(advance, rows, cols, low), out_shape=[pl...]
where the time goes in v8:
time: 20.6 us; the launch traced here: 20.5 us
  Pallas kernels  20.5 us (100%)
    pallas_call x1, Pallas kernels, shards(): pl.pallas_call(functools.partial(advance, rows, cols, low), out_shape=[pl...  18.6 us
    pallas_call x1, Pallas kernels, shards(): pl.pallas_call(place, out_shape=jax.ShapeDtypeStruct((10, 3, placed * 128...  1.89 us

profile of v8, /device:TPU:1, one launch (start us, length us, event | category | flops | bytes accessed | tf_op | source)
XLA Modules:
  0.0 20.5 jit_solution(12973239738908732613)
XLA Ops:
  0.0 18.6 %advance.1 = (f32[1624,128]{1,0:T(8,128)S(1)}, s32[72,128]{1,0:T(8,128)S(1)}, bf16[144,128]{1,0:T(8,128)(2,1)S(1)}, f32[8,128]{1,0:T(8,128)S(1)}) custom-call(f32[10,3,4096]{2,1,0:T(4,128)} %bitcast.7, f32[4,4096]{1,0:T(4,128)} %metric.1, f32[32,128]{1,0:T(8,128)} %bitcast.8, s32[32,128]{1,0:T(8,128)} %bitcast.9, s32[32,128]{1,0:T(8,128)} %bitcast.10, ...), custom_call_target="tpu_custom_call" | custom-call | tf_op jit(solution)/shard_map/advance/pallas_call | solution.py:605
  18.6 1.9 %place.1 = f32[10,3,6144]{2,1,0:T(4,128)} custom-call(s32[72,128]{1,0:T(8,128)S(1)} %get-tuple-element.9.tab, bf16[144,128]{1,0:T(8,128)(2,1)S(1)} %get-tuple-element.10.pw, f32[8,128]{1,0:T(8,128)S(1)} %get-tuple-element.11.stat, f32[1624,128]{1,0:T(8,128)S(1)} %get-tuple-element.12.st), custom_call_target="tpu_custom_call" | custom-call | tf_op jit(solution)/shard_map/place/pallas_call | solution.py:648

commit v9 on v8

--- a/solution.py
+++ b/solution.py
@@ -454,6 +454,7 @@
 
 
 def child_weights(prolong, pw, tmp, wf):
+    halves = []
     for i in range(3):
         wf[...] = jnp.zeros_like(wf)
         tmp[...] = jnp.zeros_like(tmp)
@@ -469,7 +470,15 @@
         w = wf[...]
         hi = w.astype(bf16).astype(f32)
         low = w - hi
-        pw[i * 48 : i * 48 + 48, :] = (hi + pltpu.roll(hi, 32, 1) + pltpu.roll(low, 64, 1)).astype(bf16)
+        halves += [hi, low]
+    eye, _, one, one_low, two, two_low = halves
+    first = (eye, eye, one, one)
+    rest = (one_low, two, two, two_low)
+    for k, four in enumerate((first, rest)):
+        total = four[0]
+        for j in range(1, 4):
+            total = total + pltpu.roll(four[j], 32 * j, 1)
+        pw[:, 128 * k : 128 * k + 128] = total.astype(bf16)
 
 
 def combine(m, to, step, qt, r1, r2, st):
@@ -551,7 +560,7 @@
 
 def place(tab, pw, stat, st, out, new_tiles, near, code, lidx, sems):
     tiles = aligned(stat[0:1, :], tab, near, code, lidx)
-    weight = pw[:, 0:96]
+    weight = pw[...]
     stores = []
     for pair in range(24):
         parts = []
@@ -563,13 +572,18 @@
             low = idx & 127
             s = jnp.where(idx < 128, pick(near_tile, low), pick(far_tile, low))
             hi, lo = split(s)
-            parts.append(jnp.concatenate([hi, lo, hi], axis=0))
+            kind = jnp.broadcast_to(code[r : r + 1, :], (16, 128))
+            rows = []
+            for j in range(3):
+                only = jnp.where(kind == j, 1.0, 0.0).astype(bf16)
+                only = jnp.concatenate([only, only], axis=0)
+                rows += [hi * only, lo * only]
+            rows = rows[0:4] + [rows[2]] + rows[4:6] + [rows[4]]
+            parts.append(jnp.concatenate(rows, axis=0))
         res = jnp.dot(weight, jnp.concatenate(parts, axis=1), preferred_element_type=f32)
         for i in range(2):
             r = 2 * pair + i
-            one = res[:, 128 * i : 128 * i + 128]
-            kind = jnp.broadcast_to(code[r : r + 1, :], (48, 128))
-            new = jnp.where(kind == 0, one[0:48], jnp.where(kind == 1, one[48:96], one[96:144]))
+            new = res[:, 128 * i : 128 * i + 128]
             for n in range(10):
                 new_tiles[n, :, r * 128 : (r + 1) * 128] = new[4 * n : 4 * n + 3]
         if pair in (7, 15, 20, 23):
@@ -607,7 +621,7 @@
             out_shape=[
                 pltpu.VMEM((((placed + 1) * RP + 7) // 8 * 8, 128), f32),
                 pltpu.VMEM((72, 128), i32),
-                pltpu.VMEM((144, 128), bf16),
+                pltpu.VMEM((48, 256), bf16),
                 pltpu.VMEM((8, 128), f32),
             ],
             in_specs=[hbm] * 8,

time: 20.6 us -> 20.5 us (level)
  no operation moved by 1% of the time
where the time goes in v9:
time: 20.5 us; the launch traced here: 20.4 us
  Pallas kernels  20.4 us (100%)
    pallas_call x1, Pallas kernels, shards(): pl.pallas_call(functools.partial(advance, rows, cols, low), out_shape=[pl...  18.6 us
    pallas_call x1, Pallas kernels, shards(): pl.pallas_call(place, out_shape=jax.ShapeDtypeStruct((10, 3, placed * 128...  1.81 us

profile of v9, /device:TPU:1, one launch (start us, length us, event | category | flops | bytes accessed | tf_op | source)
XLA Modules:
  0.0 20.4 jit_solution(12831587405790387371)
XLA Ops:
  0.0 18.6 %advance.1 = (f32[1624,128]{1,0:T(8,128)S(1)}, s32[72,128]{1,0:T(8,128)S(1)}, bf16[48,256]{1,0:T(8,128)(2,1)S(1)}, f32[8,128]{1,0:T(8,128)S(1)}) custom-call(f32[10,3,4096]{2,1,0:T(4,128)} %bitcast.7, f32[4,4096]{1,0:T(4,128)} %metric.1, f32[32,128]{1,0:T(8,128)} %bitcast.8, s32[32,128]{1,0:T(8,128)} %bitcast.9, s32[32,128]{1,0:T(8,128)} %bitcast.10, ...), custom_call_target="tpu_custom_call" | custom-call | tf_op jit(solution)/shard_map/advance/pallas_call | solution.py:619
  18.6 1.8 %place.1 = f32[10,3,6144]{2,1,0:T(4,128)} custom-call(s32[72,128]{1,0:T(8,128)S(1)} %get-tuple-element.9.tab, bf16[48,256]{1,0:T(8,128)(2,1)S(1)} %get-tuple-element.10.pw, f32[8,128]{1,0:T(8,128)S(1)} %get-tuple-element.11.stat, f32[1624,128]{1,0:T(8,128)S(1)} %get-tuple-element.12.st), custom_call_target="tpu_custom_call" | custom-call | tf_op jit(solution)/shard_map/place/pallas_call | solution.py:662
